TPU v7x, 32 devices: a whole 2x2x4 slice. The times are simulated.
32 devices in a mesh: chan: 8 (over z, x), bl: 4 (over y, core).
Axes of the slice: x: 2, y: 2, z: 4, core: 2. Of those that a mesh axis runs over, the one named last changes fastest.
Arguments:
- visibilities: bfloat16 [1024, 1536, 2, 128], P('bl', 'chan'), may hold values from -6 to 6
- kernels: bfloat16 [64, 128, 256], replicated, may hold values from -0.1875 to 0.1875
- block_ids: int32 [4, 64, 8], P('bl'), may hold values from 0 to 255
- kernel_ids: int32 [4, 64, 8], P('bl'), may hold values from 0 to 63
- tile_counts: int32 [4, 64], P('bl'), may hold values from 1 to 8, as said below
- wedge_mask: int32 [64, 1536], P(('chan', 'bl')), may hold values 0 or 1
Outputs:
- delay_tiles: float32 [64, 2, 256, 1536], P(('chan', 'bl'))
Inputs may be any that keep to these rules, and one draw needn't show every extreme that they name: `tile_counts`: slots at or past a tile's count are ignored; in every group some tile uses all 8 slots.
All inputs are finite; a program needn't handle non-finite values. No bound on the sum of `wedge_mask` on one device may be relied on, other than what follows from the above.
Results may differ from a plain program's by a relative error of at most 0.0095.
Values may be sent and summed in bfloat16 or wider, within the bound.
No kernel may reach another device: no remote copies, remote signals or barrier semaphores. Data moves between devices by JAX's collectives and lax.ppermute only.
A program may use at most 192 MiB of HBM per device.

v0:
```python
import functools
import math

import jax
import jax.numpy as jnp
import numpy as np
from jax import lax
from jax.experimental import pallas as pl
from jax.experimental.pallas import tpu as pltpu
from jax.sharding import PartitionSpec as P


UNIT = 16
SHARES = (1, 1)
DIRECT = (True, True, True, True)
PER = 2
RADIX = 4
LANES = 128


def piece_channels(ch_dev):
    units = ch_dev // UNIT
    ends = [round(units * sum(SHARES[: i + 1]) / sum(SHARES)) for i in range(len(SHARES))]
    return [(b - a) * UNIT for a, b in zip([0] + ends[:-1], ends)]


def after(x, *before):
    return lax.optimization_barrier((x,) + before)[0]


def xor_pairs(n, bit):
    return [(i, i ^ bit) for i in range(n)]


def grid_kernel(inner, owned, n_bl, off, flip, depth, lists_ref, vis, ker, out_ref):
    n_chan, rows = out_ref.shape[1:3]
    per = math.gcd(PER, n_chan)
    blocks = n_chan // per

    def step(g, _):
        half = g // blocks
        owner = lists_ref[2 * depth + 1, 0] ^ jnp.where(half == 0, 2, 0) ^ flip
        for i in range(per):
            chan = (g % blocks) * per + i
            tile = (chan * n_bl + owner) * owned + inner
            count = lists_ref[2 * depth, tile]
            lhs = [vis[lists_ref[k, tile], pl.ds(off, rows)] for k in range(depth)]
            lhs = [jnp.where(k < count, v, jnp.zeros_like(v)) for k, v in enumerate(lhs)]
            rhs = [ker[lists_ref[depth + k, tile]] for k in range(depth)]
            acc = jnp.dot(
                jnp.concatenate(lhs, axis=1), jnp.concatenate(rhs, axis=0), preferred_element_type=jnp.float32
            )
            out_ref[half, chan] = acc.astype(jnp.bfloat16)
        return 0

    lax.fori_loop(0, 2 * blocks, step, 0)


def grid_call(lists, vis, ker, inner, off, ch, n_chan, n_bl, owned, flip):
    vmem = pl.BlockSpec(memory_space=pltpu.VMEM)
    smem = pl.BlockSpec(memory_space=pltpu.SMEM)
    return pl.pallas_call(
        functools.partial(grid_kernel, inner, owned, n_bl, 2 * off, flip, (lists.shape[0] - 2) // 2),
        in_specs=[smem] + [vmem] * 2,
        out_specs=vmem,
        out_shape=jax.ShapeDtypeStruct((2, n_chan, 2 * ch, ker.shape[2]), jnp.bfloat16),
        compiler_params=pltpu.CompilerParams(vmem_limit_bytes=4 << 20),
    )(lists, vis, ker)


def pair_up(a, b):
    return (a.astype(jnp.float32) + b.astype(jnp.float32)).astype(jnp.bfloat16)


def sum_all(*parts):
    total = parts[0].astype(jnp.float32)
    for part in parts[1:]:
        total = total + part.astype(jnp.float32)
    return total.astype(jnp.bfloat16)


def sum_kernel(me_ref, keep_ref, near_ref, far_ref, *outs):
    for r, out in enumerate(outs):
        chan = me_ref[1] ^ r
        out[...] = sum_all(keep_ref[0, chan], near_ref[0, chan], far_ref[chan])


def sum_call(me, keep, near, far):
    _, n_chan, rows, cells = keep.shape
    half = pl.BlockSpec((1, n_chan, rows, cells), lambda i, *_: (1, 0, 0, 0))
    return pl.pallas_call(
        sum_kernel,
        grid_spec=pltpu.PrefetchScalarGridSpec(
            num_scalar_prefetch=1,
            grid=(1,),
            in_specs=[half, half, pl.BlockSpec((n_chan, rows, cells), lambda i, *_: (0, 0, 0))],
            out_specs=[pl.BlockSpec((rows, cells), lambda i, *_: (0, 0))] * n_chan,
        ),
        out_shape=[jax.ShapeDtypeStruct((rows, cells), jnp.bfloat16)] * n_chan,
        compiler_params=pltpu.CompilerParams(dimension_semantics=("arbitrary",), vmem_limit_bytes=12 << 20),
    )(me, keep, near, far)


def angle_tables(n_chan, ch_dev):
    nchan = n_chan * ch_dev
    delay = np.arange(nchan // RADIX, dtype=np.int64)
    start = np.arange(n_chan, dtype=np.int64)[:, None] * ch_dev
    inside = np.arange(ch_dev, dtype=np.int64).reshape(ch_dev // RADIX, RADIX).T[:, :, None]
    turn = lambda c: 2.0 * np.pi * (c * delay % nchan) / nchan
    return [jnp.asarray(f(turn(c)).astype(np.float32)) for c in (start, inside) for f in (np.cos, np.sin)]


def table_kernel(places, uc_ref, us_ref, vc_ref, vs_ref, *rest):
    n = len(places)
    outs, scratch = rest[:n], rest[n:]
    n_src = uc_ref.shape[0]
    for j, (off, ch) in enumerate(places):
        q = ch // RADIX
        cos, sin = scratch[2 * j], scratch[2 * j + 1]
        for m in range(RADIX):
            vc = vc_ref[m, pl.ds(off // RADIX, q), :]
            vs = vs_ref[m, pl.ds(off // RADIX, q), :]
            for r in range(n_src):
                uc = uc_ref[pl.ds(r, 1), :]
                us = us_ref[pl.ds(r, 1), :]
                cos[pl.ds(r * q, q), :] = uc * vc - us * vs
                sin[pl.ds(r * q, q), :] = us * vc + uc * vs
            k = n_src * q
            c = cos[...]
            s = sin[...]
            outs[j][0, m, pl.ds(0, k), pl.ds(0, LANES)] = c.astype(jnp.bfloat16)
            outs[j][0, m, pl.ds(0, k), pl.ds(LANES, LANES)] = (-s).astype(jnp.bfloat16)
            outs[j][0, m, pl.ds(k, k), pl.ds(0, LANES)] = s.astype(jnp.bfloat16)
            outs[j][0, m, pl.ds(k, k), pl.ds(LANES, LANES)] = c.astype(jnp.bfloat16)


def table_call(gate, sizes, n_chan, ch_dev):
    tables = angle_tables(n_chan, ch_dev)
    tables[0] = after(tables[0], gate)
    steps = tables[0].shape[-1] // LANES
    places, off = [], 0
    for ch in sizes:
        places.append((off, ch))
        off += ch
    spec = lambda t: pl.BlockSpec(t.shape[:-1] + (LANES,), lambda d, *_: (0,) * (t.ndim - 1) + (d,))
    return pl.pallas_call(
        functools.partial(table_kernel, places),
        grid=(steps,),
        in_specs=[spec(t) for t in tables],
        out_specs=[
            pl.BlockSpec((1, RADIX, 2 * n_chan * ch // RADIX, 2 * LANES), lambda d: (d, 0, 0, 0)) for ch in sizes
        ],
        scratch_shapes=[
            pltpu.VMEM((n_chan * ch // RADIX, LANES), jnp.float32) for ch in sizes for _ in range(2)
        ],
        out_shape=[
            jax.ShapeDtypeStruct((steps, RADIX, 2 * n_chan * ch // RADIX, 2 * LANES), jnp.bfloat16)
            for ch in sizes
        ],
        compiler_params=pltpu.CompilerParams(dimension_semantics=("arbitrary",), vmem_limit_bytes=12 << 20),
        name="tables",
    )(*tables)


def turn_kernel(counts, has_acc, inner, scale, me_ref, *refs):
    final = inner is not None
    rest = list(refs)
    gs = [[rest.pop(0) for _ in range(c)] for c in counts]
    ts = [rest.pop(0) for _ in counts]
    acc_ref = rest.pop(0) if has_acc else None
    if final:
        mask_ref, _, out_hbm, turned, stage, bins, sems = rest
    else:
        out_ref, turned, stage = rest
    d = pl.program_id(0)
    steps = pl.num_programs(0)

    @pl.when(d == 0)
    def _():
        at = 0
        for g in gs:
            if len(g) == 1:
                n_src, rows, _ = g[0].shape
            else:
                n_src, rows = len(g), g[0].shape[0]
            for r in range(n_src):
                for h in range(stage.shape[0]):
                    lanes = pl.ds(h * LANES, LANES)
                    if len(g) == 1:
                        stage[h, pl.ds(r * rows, rows), :] = g[0][r, :, lanes].astype(jnp.float32)
                    else:
                        start = pl.multiple_of((me_ref[1] ^ r) * rows, 8)
                        stage[h, pl.ds(start, rows), :] = g[r][:, lanes].astype(jnp.float32)
            k = n_src * rows // (2 * RADIX)
            for m in range(RADIX):
                for h in range(stage.shape[0]):
                    parts = [
                        stage[h, pl.ds(2 * m + p, k, stride=2 * RADIX), :].astype(jnp.bfloat16) for p in range(2)
                    ]
                    turned[m, pl.ds(h * LANES, LANES), pl.ds(at, 2 * k)] = jnp.concatenate(parts, axis=0).T
            at += 2 * k

    sums = []
    for m in range(RADIX):
        at = 0
        total = None
        for t in ts:
            k = t.shape[2]
            part = jnp.dot(turned[m, :, pl.ds(at, k)], t[0, m], preferred_element_type=jnp.float32)
            total = part if total is None else total + part
            at += k
        if has_acc:
            total = total + acc_ref[0, m]
        sums.append(total)
    if not final:
        for m in range(RADIX):
            out_ref[0, m] = sums[m]
        return

    def copies(step):
        slot = step % 2
        width = steps * LANES
        return [
            pltpu.make_async_copy(
                bins.at[slot, j],
                out_hbm.at[inner, :, :, pl.ds(pl.multiple_of(j * width + step * LANES, LANES), LANES)],
                sems.at[slot, j],
            )
            for j in range(RADIX)
        ]

    @pl.when(d >= 2)
    def _():
        for c in copies(d - 2):
            c.wait()

    re = [s[:, :LANES] for s in sums]
    im = [s[:, LANES:] for s in sums]
    e0r, e0i, e1r, e1i = re[0] + re[2], im[0] + im[2], re[0] - re[2], im[0] - im[2]
    o0r, o0i, o1r, o1i = re[1] + re[3], im[1] + im[3], re[1] - re[3], im[1] - im[3]
    joined = (
        (e0r + o0r, e0i + o0i),
        (e1r + o1i, e1i - o1r),
        (e0r - o0r, e0i - o0i),
        (e1r - o1i, e1i + o1r),
    )
    slot = d % 2
    for j, parts in enumerate(joined):
        at = pl.ds(pl.multiple_of((j * steps + d) * LANES, LANES), LANES)
        keep = mask_ref[pl.ds(inner, 1), at].astype(jnp.float32) * scale
        for p, value in enumerate(parts):
            bins[slot, j, p] = value * keep
    for c in copies(d):
        c.start()

    @pl.when(d == steps - 1)
    def _():
        for back in range(min(2, out_hbm.shape[3] // (RADIX * LANES)) - 1, -1, -1):
            for c in copies(d - back):
                c.wait()


def turn_call(me, gs, ts, acc, mask, out, inner):
    cells = gs[0][0].shape[-1]
    steps = ts[0].shape[0]
    final = inner is not None
    has_acc = acc is not None
    k = sum(t.shape[2] for t in ts)
    whole = lambda a: pl.BlockSpec(a.shape, lambda d, *_: (0,) * a.ndim, pipeline_mode=pl.Buffered(1))
    acc_spec = pl.BlockSpec((1, RADIX, cells, 2 * LANES), lambda d, *_: (d, 0, 0, 0))
    ins = [a for g in gs for a in g]
    specs = [whole(a) for a in ins]
    ins += ts
    specs += [pl.BlockSpec((1,) + t.shape[1:], lambda d, *_: (d, 0, 0, 0)) for t in ts]
    if has_acc:
        ins.append(acc)
        specs.append(acc_spec)
    scratch = [
        pltpu.VMEM((RADIX, cells, k), jnp.bfloat16),
        pltpu.VMEM((cells // LANES, max(sum(a.size for a in g) for g in gs) // cells, LANES), jnp.float32),
    ]
    if final:
        alias = {len(ins) + 2: 0}
        ins += [mask, out]
        specs += [whole(mask), pl.BlockSpec(memory_space=pltpu.HBM)]
        out_spec = pl.BlockSpec(memory_space=pltpu.HBM)
        out_shape = jax.ShapeDtypeStruct(out.shape, out.dtype)
        scratch += [
            pltpu.VMEM((2, RADIX, 2, cells, LANES), jnp.float32),
            pltpu.SemaphoreType.DMA((2, RADIX)),
        ]
    else:
        alias = {}
        out_spec = acc_spec
        out_shape = jax.ShapeDtypeStruct((steps, RADIX, cells, 2 * LANES), jnp.float32)
    nchan = steps * RADIX * LANES
    return pl.pallas_call(
        functools.partial(turn_kernel, [len(g) for g in gs], has_acc, inner, 1.0 / math.sqrt(nchan)),
        grid_spec=pltpu.PrefetchScalarGridSpec(
            num_scalar_prefetch=1,
            grid=(steps,),
            in_specs=specs,
            out_specs=out_spec,
            scratch_shapes=scratch,
        ),
        out_shape=out_shape,
        input_output_aliases=alias,
        compiler_params=pltpu.CompilerParams(dimension_semantics=("arbitrary",), vmem_limit_bytes=14 << 20),
    )(me, *ins)


def empty_kernel(out_ref):
    pass


def empty(shape):
    return pl.pallas_call(
        empty_kernel,
        out_specs=pl.BlockSpec(memory_space=pltpu.HBM),
        out_shape=jax.ShapeDtypeStruct(shape, jnp.float32),
        compiler_params=pltpu.CompilerParams(vmem_limit_bytes=1 << 20),
        name="empty",
    )()


def local(visibilities, kernels, block_ids, kernel_ids, tile_counts, wedge_mask):
    n_chan = lax.axis_size("chan")
    n_bl = lax.axis_size("bl")
    nblocks, ch_dev, _, block_len = visibilities.shape
    cells = kernels.shape[2]
    owned = wedge_mask.shape[0]
    nchan = ch_dev * n_chan
    vis = visibilities.reshape(nblocks, ch_dev * 2, block_len)
    me = jnp.stack([lax.axis_index("bl"), lax.axis_index("chan")]).astype(jnp.int32)
    place = jnp.full((1, tile_counts.shape[1]), me[0], jnp.int32)
    lists = jnp.concatenate([block_ids[0].T, kernel_ids[0].T, tile_counts, place], axis=0)
    sizes = piece_channels(ch_dev)
    n = len(sizes)
    starts = [sum(sizes[:j]) for j in range(n)]
    blocks = []
    for inner in range(owned):
        blocks += [(inner, j) for j in (range(n) if inner < owned - 1 else range(n - 1, -1, -1))]
    keep, near, sent, far, total, arrived = {}, {}, {}, {}, {}, {}
    tables = out = acc = None
    gate = me

    for what, i in order_of_work(len(blocks)):
        if what in ("give", "grid"):
            inner, j = blocks[i]
            part = grid_call(
                after(lists, gate), vis, kernels,
                inner, starts[j], sizes[j], n_chan, n_bl, owned, int(what == "give"),
            )
            gate = part
            if what == "grid":
                keep[i] = part
            else:
                near[i] = lax.ppermute(part, "bl", xor_pairs(n_bl, 1))
        elif what == "tables":
            tables = table_call(gate, sizes, n_chan, ch_dev)
            gate = tables[0]
        elif what == "pair":
            gate = sent[i] = pair_up(after(keep[i], gate)[0], near[i][0])
            far[i] = lax.ppermute(sent[i], "bl", xor_pairs(n_bl, 2))
        elif what == "sum":
            if DIRECT[i % len(DIRECT)]:
                total[i] = sum_call(me, after(keep[i], gate), near[i], far[i])
                gate = total[i][0]
            else:
                gate = total[i] = sum_all(after(keep[i], gate)[1], near[i][1], far[i])
        elif what == "spread":
            if DIRECT[i % len(DIRECT)]:
                arrived[blocks[i]] = [total[i][0]] + [
                    lax.ppermute(total[i][r], "chan", xor_pairs(n_chan, r)) for r in range(1, n_chan)
                ]
            else:
                arrived[blocks[i]] = [lax.all_to_all(total[i], "chan", 0, 0, tiled=True)]
        elif what == "join":
            if out is None:
                out = empty((owned, 2, cells, nchan))
            if i < owned - 1:
                got, last = [(i, j) for j in range(n)], True
            elif n > 1 and i == owned - 1:
                got, last = blocks[-n:-1], False
            else:
                got, last = blocks[-1:], True
            gs = [arrived[key] for key in got]
            gs[0] = [after(gs[0][0], gate)] + gs[0][1:]
            ts = [tables[j] for _, j in got]
            if last:
                gate = out = turn_call(me, gs, ts, acc, wedge_mask, out, got[0][0])
            else:
                gate = acc = turn_call(me, gs, ts, None, None, None, None)
    return out


ORDER = (
    ("give", 0), ("grid", 0), ("pair", 0), ("give", 1), ("grid", 1), ("give", 2), ("pair", 1), ("grid", 2),
    ("pair", 2), ("sum", 0), ("spread", 0), ("give", 3), ("sum", 1), ("spread", 1), ("grid", 3), ("pair", 3),
    ("sum", 2), ("spread", 2), ("tables", 0), ("sum", 3), ("spread", 3), ("join", 0), ("join", 1), ("join", 2),
)


def order_of_work(n):
    if n == 4 and len(SHARES) == 2:
        return ORDER
    work = [("tables", 0)]
    for i in range(n):
        work += [("give", i), ("grid", i), ("pair", i)]
    for i in range(n):
        work += [("sum", i), ("spread", i)]
    tiles = n // len(SHARES)
    return work + [("join", i) for i in range(tiles + (len(SHARES) > 1))]


def solution(mesh):
    return jax.shard_map(
        local,
        mesh=mesh,
        in_specs=(
            P("bl", "chan", None, None),
            P(),
            P("bl", None, None),
            P("bl", None, None),
            P("bl", None),
            P(("chan", "bl"), None),
        ),
        out_specs=P(("chan", "bl"), None, None, None),
        check_vma=False,
    )
```

profile of v0, /device:TPU:0, one launch (start us, length us, event | category | flops | bytes accessed | tf_op | source)
XLA Modules:
  0.0 170.2 jit_solution(5976827421338463117)
XLA Ops:
  0.1 0.8 add_add_fusion.lists_ref
  0.9 8.2 %copy-done = bf16[256,192,2,128]{3,2,1,0:T(2,128)(2,1)S(1)} copy-done((bf16[256,192,2,128]{3,2,1,0:T(2,128)(2,1)S(1)}, bf16[256,192,2,128]{3,2,1,0:T(2,128)(2,1)}, u32[]{:S(2)}) %copy-start) | copy-done | bytes 25165848
  9.1 2.2 %copy-done.1 = bf16[64,128,256]{2,1,0:T(8,128)(2,1)S(1)} copy-done((bf16[64,128,256]{2,1,0:T(8,128)(2,1)S(1)}, bf16[64,128,256]{2,1,0:T(8,128)(2,1)}, u32[]{:S(2)}) %copy-start.1) | copy-done | bytes 4194328
  11.3 3.8 %shard_map.100 = bf16[2,8,192,256]{3,2,1,0:T(8,128)(2,1)S(1)} custom-call(s32[18,64]{1,0:T(8,128)S(1)} %add_add_fusion.lists_ref, bf16[256,384,128]{2,1,0:T(8,128)(2,1)S(1)} %bitcast.18, bf16[64,128,256]{2,1,0:T(8,128)(2,1)S(1)} %copy-done.1), custom_call_target="tpu_custom_call" | custom-call | tf_op jit(solution)/shard_map/pallas_call | solution.py:62
  15.7 3.8 %shard_map.101.keep_ref = bf16[2,8,192,256]{3,2,1,0:T(8,128)(2,1)S(1)} custom-call(s32[18,64]{1,0:T(8,128)S(1)} %add_add_fusion.lists_ref, bf16[256,384,128]{2,1,0:T(8,128)(2,1)S(1)} %bitcast.19, bf16[64,128,256]{2,1,0:T(8,128)(2,1)S(1)} %copy-done.1), custom_call_target="tpu_custom_call" | custom-call | tf_op jit(solution)/shard_map/pallas_call | solution.py:62
  19.9 3.8 %shard_map.102 = bf16[2,8,192,256]{3,2,1,0:T(8,128)(2,1)S(1)} custom-call(s32[18,64]{1,0:T(8,128)S(1)} %add_add_fusion.lists_ref, bf16[256,384,128]{2,1,0:T(8,128)(2,1)S(1)} %bitcast.22, bf16[64,128,256]{2,1,0:T(8,128)(2,1)S(1)} %copy-done.1), custom_call_target="tpu_custom_call" | custom-call | tf_op jit(solution)/shard_map/pallas_call | solution.py:62
  24.3 3.8 %shard_map.103.keep_ref = bf16[2,8,192,256]{3,2,1,0:T(8,128)(2,1)S(1)} custom-call(s32[18,64]{1,0:T(8,128)S(1)} %add_add_fusion.lists_ref, bf16[256,384,128]{2,1,0:T(8,128)(2,1)S(1)} %bitcast.23, bf16[64,128,256]{2,1,0:T(8,128)(2,1)S(1)} %copy-done.1), custom_call_target="tpu_custom_call" | custom-call | tf_op jit(solution)/shard_map/pallas_call | solution.py:62
  28.2 3.8 %shard_map.104 = bf16[2,8,192,256]{3,2,1,0:T(8,128)(2,1)S(1)} custom-call(s32[18,64]{1,0:T(8,128)S(1)} %add_add_fusion.lists_ref, bf16[256,384,128]{2,1,0:T(8,128)(2,1)S(1)} %bitcast.24, bf16[64,128,256]{2,1,0:T(8,128)(2,1)S(1)} %copy-done.1), custom_call_target="tpu_custom_call" | custom-call | tf_op jit(solution)/shard_map/pallas_call | solution.py:62
  32.1 3.0 %collective-permute-start.3 = (bf16[8,192,256]{2,1,0:T(8,128)(2,1)S(1)}, bf16[8,192,256]{2,1,0:T(8,128)(2,1)S(1)}, u32[]{:S(2)}, u32[]{:S(2)}) collective-permute-start(bf16[8,192,256]{2,1,0:T(8,128)(2,1)S(1)} %fusion), channel_id=1, source_target_pairs={{0,2},{1,3},{2,0},{3,1},{4,6},{5,7},{6,4},{7,5},{8,10},{9,11},{10,... | collective-permute-start | bytes 2359304 | tf_op jit(solution)/shard_map/ppermute | solution.py:364
  35.3 3.8 %shard_map.105.keep_ref = bf16[2,8,192,256]{3,2,1,0:T(8,128)(2,1)S(1)} custom-call(s32[18,64]{1,0:T(8,128)S(1)} %add_add_fusion.lists_ref, bf16[256,384,128]{2,1,0:T(8,128)(2,1)S(1)} %bitcast.25, bf16[64,128,256]{2,1,0:T(8,128)(2,1)S(1)} %copy-done.1), custom_call_target="tpu_custom_call" | custom-call | tf_op jit(solution)/shard_map/pallas_call | solution.py:62
  39.4 13.5 %collective-permute-done.3.far_ref = bf16[8,192,256]{2,1,0:T(8,128)(2,1)S(1)} collective-permute-done((bf16[8,192,256]{2,1,0:T(8,128)(2,1)S(1)}, bf16[8,192,256]{2,1,0:T(8,128)(2,1)S(1)}, u32[]{:S(2)}, u32[]{:S(2)}) %collective-permute-start.3) | collective-permute-done | bytes 786464 | tf_op jit(solution)/shard_map/ppermute | solution.py:364
  52.9 0.8 shard_map.106
  53.7 3.8 %shard_map.107 = bf16[2,8,192,256]{3,2,1,0:T(8,128)(2,1)S(1)} custom-call(s32[18,64]{1,0:T(8,128)S(1)} %add_add_fusion.lists_ref, bf16[256,384,128]{2,1,0:T(8,128)(2,1)S(1)} %bitcast.26, bf16[64,128,256]{2,1,0:T(8,128)(2,1)S(1)} %copy-done.1), custom_call_target="tpu_custom_call" | custom-call | tf_op jit(solution)/shard_map/pallas_call | solution.py:62
  57.6 1.8 %collective-permute-start.4 = (bf16[8,192,256]{2,1,0:T(8,128)(2,1)S(1)}, bf16[8,192,256]{2,1,0:T(8,128)(2,1)S(1)}, u32[]{:S(2)}, u32[]{:S(2)}) collective-permute-start(bf16[8,192,256]{2,1,0:T(8,128)(2,1)S(1)} %fusion.1), channel_id=1, source_target_pairs={{0,2},{1,3},{2,0},{3,1},{4,6},{5,7},{6,4},{7,5},{8,10},{9,11},{10,... | collective-permute-start | bytes 2359304 | tf_op jit(solution)/shard_map/ppermute | solution.py:364
  59.7 18.4 %collective-permute-done.4.far_ref = bf16[8,192,256]{2,1,0:T(8,128)(2,1)S(1)} collective-permute-done((bf16[8,192,256]{2,1,0:T(8,128)(2,1)S(1)}, bf16[8,192,256]{2,1,0:T(8,128)(2,1)S(1)}, u32[]{:S(2)}, u32[]{:S(2)}) %collective-permute-start.4) | collective-permute-done | bytes 786464 | tf_op jit(solution)/shard_map/ppermute | solution.py:364
  78.1 0.8 shard_map.108
  78.9 3.8 %shard_map.109.keep_ref = bf16[2,8,192,256]{3,2,1,0:T(8,128)(2,1)S(1)} custom-call(s32[18,64]{1,0:T(8,128)S(1)} %add_add_fusion.lists_ref, bf16[256,384,128]{2,1,0:T(8,128)(2,1)S(1)} %bitcast.27, bf16[64,128,256]{2,1,0:T(8,128)(2,1)S(1)} %copy-done.1), custom_call_target="tpu_custom_call" | custom-call | tf_op jit(solution)/shard_map/pallas_call | solution.py:62
  83.0 1.8 %collective-permute-start.7 = (bf16[8,192,256]{2,1,0:T(8,128)(2,1)S(1)}, bf16[8,192,256]{2,1,0:T(8,128)(2,1)S(1)}, u32[]{:S(2)}, u32[]{:S(2)}) collective-permute-start(bf16[8,192,256]{2,1,0:T(8,128)(2,1)S(1)} %fusion.3), channel_id=1, source_target_pairs={{0,2},{1,3},{2,0},{3,1},{4,6},{5,7},{6,4},{7,5},{8,10},{9,11},{10,... | collective-permute-start | bytes 2359304 | tf_op jit(solution)/shard_map/ppermute | solution.py:364
  84.8 1.5 collective-permute-start.8
  86.3 1.6 collective-permute-start.9
  88.3 1.2 collective-permute-done.8.refs_1_
  89.5 2.6 %collective-permute-start.11 = (bf16[192,256]{1,0:T(8,128)(2,1)S(1)}, bf16[192,256]{1,0:T(8,128)(2,1)S(1)}, u32[]{:S(2)}, u32[]{:S(2)}) collective-permute-start(bf16[192,256]{1,0:T(8,128)(2,1)S(1)} %get-tuple-element.85), channel_id=1, source_target_pairs={{0,16},{4,20},{8,24},{12,28},{16,0},{20,4},{24,8},{28,12},{1,17},{... | collective-permute-start | bytes 294920 | tf_op jit(solution)/shard_map/ppermute | solution.py:374
  92.1 2.4 %collective-permute-start.12 = (bf16[192,256]{1,0:T(8,128)(2,1)S(1)}, bf16[192,256]{1,0:T(8,128)(2,1)S(1)}, u32[]{:S(2)}, u32[]{:S(2)}) collective-permute-start(bf16[192,256]{1,0:T(8,128)(2,1)S(1)} %get-tuple-element.86), channel_id=1, source_target_pairs={{0,20},{4,16},{8,28},{12,24},{16,4},{20,0},{24,12},{28,8},{1,21},{... | collective-permute-start | bytes 294920 | tf_op jit(solution)/shard_map/ppermute | solution.py:374
  94.5 3.4 %collective-permute-start.13 = (bf16[192,256]{1,0:T(8,128)(2,1)S(1)}, bf16[192,256]{1,0:T(8,128)(2,1)S(1)}, u32[]{:S(2)}, u32[]{:S(2)}) collective-permute-start(bf16[192,256]{1,0:T(8,128)(2,1)S(1)} %get-tuple-element.87), channel_id=1, source_target_pairs={{0,24},{4,28},{8,16},{12,20},{16,8},{20,12},{24,0},{28,4},{1,25},{... | collective-permute-start | bytes 294920 | tf_op jit(solution)/shard_map/ppermute | solution.py:374
  98.0 4.3 %collective-permute-done.11.refs_4_ = bf16[192,256]{1,0:T(8,128)(2,1)S(1)} collective-permute-done((bf16[192,256]{1,0:T(8,128)(2,1)S(1)}, bf16[192,256]{1,0:T(8,128)(2,1)S(1)}, u32[]{:S(2)}, u32[]{:S(2)}) %collective-permute-start.11) | collective-permute-done | bytes 98336 | tf_op jit(solution)/shard_map/ppermute | solution.py:374
  102.3 3.8 %collective-permute-start.14 = (bf16[192,256]{1,0:T(8,128)(2,1)S(1)}, bf16[192,256]{1,0:T(8,128)(2,1)S(1)}, u32[]{:S(2)}, u32[]{:S(2)}) collective-permute-start(bf16[192,256]{1,0:T(8,128)(2,1)S(1)} %get-tuple-element.88), channel_id=1, source_target_pairs={{0,28},{4,24},{8,20},{12,16},{16,12},{20,8},{24,4},{28,0},{1,29},{... | collective-permute-start | bytes 294920 | tf_op jit(solution)/shard_map/ppermute | solution.py:374
  107.0 3.2 %collective-permute-done.14.refs_7_ = bf16[192,256]{1,0:T(8,128)(2,1)S(1)} collective-permute-done((bf16[192,256]{1,0:T(8,128)(2,1)S(1)}, bf16[192,256]{1,0:T(8,128)(2,1)S(1)}, u32[]{:S(2)}, u32[]{:S(2)}) %collective-permute-start.14) | collective-permute-done | bytes 98336 | tf_op jit(solution)/shard_map/ppermute | solution.py:374
  110.3 3.9 %collective-permute-start.18 = (bf16[192,256]{1,0:T(8,128)(2,1)S(1)}, bf16[192,256]{1,0:T(8,128)(2,1)S(1)}, u32[]{:S(2)}, u32[]{:S(2)}) collective-permute-start(bf16[192,256]{1,0:T(8,128)(2,1)S(1)} %get-tuple-element.92), channel_id=1, source_target_pairs={{0,16},{4,20},{8,24},{12,28},{16,0},{20,4},{24,8},{28,12},{1,17},{... | collective-permute-start | bytes 294920 | tf_op jit(solution)/shard_map/ppermute | solution.py:374
  114.2 2.4 %collective-permute-start.20 = (bf16[192,256]{1,0:T(8,128)(2,1)S(1)}, bf16[192,256]{1,0:T(8,128)(2,1)S(1)}, u32[]{:S(2)}, u32[]{:S(2)}) collective-permute-start(bf16[192,256]{1,0:T(8,128)(2,1)S(1)} %get-tuple-element.94), channel_id=1, source_target_pairs={{0,24},{4,28},{8,16},{12,20},{16,8},{20,12},{24,0},{28,4},{1,25},{... | collective-permute-start | bytes 294920 | tf_op jit(solution)/shard_map/ppermute | solution.py:374
  116.6 0.8 shard_map.110
  117.5 3.5 %collective-permute-start.21 = (bf16[192,256]{1,0:T(8,128)(2,1)S(1)}, bf16[192,256]{1,0:T(8,128)(2,1)S(1)}, u32[]{:S(2)}, u32[]{:S(2)}) collective-permute-start(bf16[192,256]{1,0:T(8,128)(2,1)S(1)} %get-tuple-element.95), channel_id=1, source_target_pairs={{0,28},{4,24},{8,20},{12,16},{16,12},{20,8},{24,4},{28,0},{1,29},{... | collective-permute-start | bytes 294920 | tf_op jit(solution)/shard_map/ppermute | solution.py:374
  121.0 2.8 %collective-permute-done.18.refs_12_ = bf16[192,256]{1,0:T(8,128)(2,1)S(1)} collective-permute-done((bf16[192,256]{1,0:T(8,128)(2,1)S(1)}, bf16[192,256]{1,0:T(8,128)(2,1)S(1)}, u32[]{:S(2)}, u32[]{:S(2)}) %collective-permute-start.18) | collective-permute-done | bytes 98336 | tf_op jit(solution)/shard_map/ppermute | solution.py:374
  124.1 2.4 %collective-permute-done.19.refs_13_ = bf16[192,256]{1,0:T(8,128)(2,1)S(1)} collective-permute-done((bf16[192,256]{1,0:T(8,128)(2,1)S(1)}, bf16[192,256]{1,0:T(8,128)(2,1)S(1)}, u32[]{:S(2)}, u32[]{:S(2)}) %collective-permute-start.19) | collective-permute-done | bytes 98336 | tf_op jit(solution)/shard_map/ppermute | solution.py:374
  126.5 2.6 %collective-permute-start.24 = (bf16[192,256]{1,0:T(8,128)(2,1)S(1)}, bf16[192,256]{1,0:T(8,128)(2,1)S(1)}, u32[]{:S(2)}, u32[]{:S(2)}) collective-permute-start(bf16[192,256]{1,0:T(8,128)(2,1)S(1)} %get-tuple-element.100), channel_id=1, source_target_pairs={{0,12},{4,8},{8,4},{12,0},{16,28},{20,24},{24,20},{28,16},{1,13},{... | collective-permute-start | bytes 294920 | tf_op jit(solution)/shard_map/ppermute | solution.py:374
  129.9 1.0 tables.1
  130.9 0.8 shard_map.111
  131.8 3.4 %collective-permute-start.26 = (bf16[192,256]{1,0:T(8,128)(2,1)S(1)}, bf16[192,256]{1,0:T(8,128)(2,1)S(1)}, u32[]{:S(2)}, u32[]{:S(2)}) collective-permute-start(bf16[192,256]{1,0:T(8,128)(2,1)S(1)} %get-tuple-element.102), channel_id=1, source_target_pairs={{0,20},{4,16},{8,28},{12,24},{16,4},{20,0},{24,12},{28,8},{1,21},{... | collective-permute-start | bytes 294920 | tf_op jit(solution)/shard_map/ppermute | solution.py:374
  135.2 1.9 %collective-permute-start.27 = (bf16[192,256]{1,0:T(8,128)(2,1)S(1)}, bf16[192,256]{1,0:T(8,128)(2,1)S(1)}, u32[]{:S(2)}, u32[]{:S(2)}) collective-permute-start(bf16[192,256]{1,0:T(8,128)(2,1)S(1)} %get-tuple-element.103), channel_id=1, source_target_pairs={{0,24},{4,28},{8,16},{12,20},{16,8},{20,12},{24,0},{28,4},{1,25},{... | collective-permute-start | bytes 294920 | tf_op jit(solution)/shard_map/ppermute | solution.py:374
  137.1 1.6 collective-permute-start.28
  138.8 1.7 collective-permute-start.29
  140.5 5.7 %collective-permute-done.26.refs_5_ = bf16[192,256]{1,0:T(8,128)(2,1)S(1)} collective-permute-done((bf16[192,256]{1,0:T(8,128)(2,1)S(1)}, bf16[192,256]{1,0:T(8,128)(2,1)S(1)}, u32[]{:S(2)}, u32[]{:S(2)}) %collective-permute-start.26) | collective-permute-done | bytes 98336 | tf_op jit(solution)/shard_map/ppermute | solution.py:374
  146.1 5.5 %collective-permute-start.32 = (bf16[192,256]{1,0:T(8,128)(2,1)S(1)}, bf16[192,256]{1,0:T(8,128)(2,1)S(1)}, u32[]{:S(2)}, u32[]{:S(2)}) collective-permute-start(bf16[192,256]{1,0:T(8,128)(2,1)S(1)} %get-tuple-element.109), channel_id=1, source_target_pairs={{0,16},{4,20},{8,24},{12,28},{16,0},{20,4},{24,8},{28,12},{1,17},{... | collective-permute-start | bytes 294920 | tf_op jit(solution)/shard_map/ppermute | solution.py:374
  151.7 3.0 %collective-permute-start.33 = (bf16[192,256]{1,0:T(8,128)(2,1)S(1)}, bf16[192,256]{1,0:T(8,128)(2,1)S(1)}, u32[]{:S(2)}, u32[]{:S(2)}) collective-permute-start(bf16[192,256]{1,0:T(8,128)(2,1)S(1)} %get-tuple-element.110), channel_id=1, source_target_pairs={{0,20},{4,16},{8,28},{12,24},{16,4},{20,0},{24,12},{28,8},{1,21},{... | collective-permute-start | bytes 294920 | tf_op jit(solution)/shard_map/ppermute | solution.py:374
  154.7 1.4 collective-permute-start.34
  156.1 2.9 %collective-permute-start.35 = (bf16[192,256]{1,0:T(8,128)(2,1)S(1)}, bf16[192,256]{1,0:T(8,128)(2,1)S(1)}, u32[]{:S(2)}, u32[]{:S(2)}) collective-permute-start(bf16[192,256]{1,0:T(8,128)(2,1)S(1)} %get-tuple-element.112), channel_id=1, source_target_pairs={{0,28},{4,24},{8,20},{12,16},{16,12},{20,8},{24,4},{28,0},{1,29},{... | collective-permute-start | bytes 294920 | tf_op jit(solution)/shard_map/ppermute | solution.py:374
  159.0 5.0 %shard_map.112.refs_11_ = f32[2,2,256,1536]{3,2,1,0:T(8,128)} custom-call(s32[2]{0:T(128)S(1)} %pad_add_fusion.me_ref, bf16[192,256]{1,0:T(8,128)(2,1)S(1)} %get-tuple-element.81.refs_0_, bf16[192,256]{1,0:T(8,128)(2,1)S(1)} %collective-permute-done.8.refs_1_, bf16[192,256]{1,0:T(8,128)(2,1)S(1)} %collective-permute-done.9.refs_2_, ...), custom_call_target="tpu_custom_call", output_to_operand_aliasing={{}: (20, {})} | custom-call | tf_op jit(solution)/shard_map/pallas_call | solution.py:297
  164.0 2.3 %shard_map.113.refs_9_ = f32[3,4,256,256]{3,2,1,0:T(8,128)S(1)} custom-call(s32[2]{0:T(128)S(1)} %pad_add_fusion.me_ref, bf16[192,256]{1,0:T(8,128)(2,1)S(1)} %get-tuple-element.97.refs_0_, bf16[192,256]{1,0:T(8,128)(2,1)S(1)} %collective-permute-done.22.refs_1_, bf16[192,256]{1,0:T(8,128)(2,1)S(1)} %collective-permute-done.23.refs_2_, ...), custom_call_target="tpu_custom_call" | custom-call | tf_op jit(solution)/shard_map/pallas_call | solution.py:297
  166.4 3.8 %shard_map.114 = f32[2,2,256,1536]{3,2,1,0:T(8,128)} custom-call(s32[2]{0:T(128)S(1)} %pad_add_fusion.me_ref, bf16[192,256]{1,0:T(8,128)(2,1)S(1)} %get-tuple-element.105.refs_0_, bf16[192,256]{1,0:T(8,128)(2,1)S(1)} %collective-permute-done.29.refs_1_, bf16[192,256]{1,0:T(8,128)(2,1)S(1)} %collective-permute-done.30.refs_2_, ...), custom_call_target="tpu_custom_call", output_to_operand_aliasing={{}: (12, {})} | custom-call | tf_op jit(solution)/shard_map/pallas_call | solution.py:297
  (75 shorter events, 5.2 us)
Async XLA Ops:
  0.9 8.2 %copy-start = (bf16[256,192,2,128]{3,2,1,0:T(2,128)(2,1)S(1)}, bf16[256,192,2,128]{3,2,1,0:T(2,128)(2,1)}, u32[]{:S(2)}) copy-start(bf16[256,192,2,128]{3,2,1,0:T(2,128)(2,1)} %param.10) | copy-start | bytes 75497472
  11.3 8.5 %slice-start = ((s8[25165824]{0:T(1024)(128)(4,1)}), s8[4194304]{0:T(1024)(128)(4,1)S(1)}, s32[]{:S(2)}) async-start(s8[25165824]{0:T(1024)(128)(4,1)} %bitcast.20), calls=%async_computation | async-start | bytes 8388608
  11.3 8.5 %slice-start.1 = ((s8[25165824]{0:T(1024)(128)(4,1)}), s8[4194304]{0:T(1024)(128)(4,1)S(1)}, s32[]{:S(2)}) async-start(s8[25165824]{0:T(1024)(128)(4,1)} %bitcast.20), calls=%async_computation.1 | async-start | bytes 8388608
  11.3 8.5 %slice-start.2 = ((s8[25165824]{0:T(1024)(128)(4,1)}), s8[4194304]{0:T(1024)(128)(4,1)S(1)}, s32[]{:S(2)}) async-start(s8[25165824]{0:T(1024)(128)(4,1)} %bitcast.20), calls=%async_computation.2 | async-start | bytes 8388608
  15.1 4.7 %slice-start.3 = ((s8[25165824]{0:T(1024)(128)(4,1)}), s8[4194304]{0:T(1024)(128)(4,1)S(1)}, s32[]{:S(2)}) async-start(s8[25165824]{0:T(1024)(128)(4,1)} %bitcast.20), calls=%async_computation.3 | async-start | bytes 8388608
  15.2 4.7 %slice-start.4 = ((s8[25165824]{0:T(1024)(128)(4,1)}), s8[4194304]{0:T(1024)(128)(4,1)S(1)}, s32[]{:S(2)}) async-start(s8[25165824]{0:T(1024)(128)(4,1)} %bitcast.20), calls=%async_computation.4 | async-start | bytes 8388608
  15.2 4.7 %slice-start.5 = ((s8[25165824]{0:T(1024)(128)(4,1)}), s8[4194304]{0:T(1024)(128)(4,1)S(1)}, s32[]{:S(2)}) async-start(s8[25165824]{0:T(1024)(128)(4,1)} %bitcast.20), calls=%async_computation.5 | async-start | bytes 8388608
  15.2 4.4 %collective-permute-start = (bf16[2,8,192,256]{3,2,1,0:T(8,128)(2,1)S(1)}, bf16[2,8,192,256]{3,2,1,0:T(8,128)(2,1)S(1)}, u32[]{:S(2)}, u32[]{:S(2)}) collective-permute-start(bf16[2,8,192,256]{3,2,1,0:T(8,128)(2,1)S(1)} %shard_map.100), channel_id=1, source_target_pairs={{0,1},{1,0},{2,3},{3,2},{4,5},{5,4},{6,7},{7,6},{8,9},{9,8},{10,11... | collective-permute-start | bytes 4718600 | tf_op jit(solution)/shard_map/ppermute | solution.py:358
  23.8 11.3 %collective-permute-start.1 = (bf16[2,8,192,256]{3,2,1,0:T(8,128)(2,1)S(1)}, bf16[2,8,192,256]{3,2,1,0:T(8,128)(2,1)S(1)}, u32[]{:S(2)}, u32[]{:S(2)}) collective-permute-start(bf16[2,8,192,256]{3,2,1,0:T(8,128)(2,1)S(1)} %shard_map.102), channel_id=1, source_target_pairs={{0,1},{1,0},{2,3},{3,2},{4,5},{5,4},{6,7},{7,6},{8,9},{9,8},{10,11... | collective-permute-start | bytes 4718600 | tf_op jit(solution)/shard_map/ppermute | solution.py:358
  32.0 7.2 %collective-permute-start.2 = (bf16[2,8,192,256]{3,2,1,0:T(8,128)(2,1)S(1)}, bf16[2,8,192,256]{3,2,1,0:T(8,128)(2,1)S(1)}, u32[]{:S(2)}, u32[]{:S(2)}) collective-permute-start(bf16[2,8,192,256]{3,2,1,0:T(8,128)(2,1)S(1)} %shard_map.104), channel_id=1, source_target_pairs={{0,1},{1,0},{2,3},{3,2},{4,5},{5,4},{6,7},{7,6},{8,9},{9,8},{10,11... | collective-permute-start | bytes 4718600 | tf_op jit(solution)/shard_map/ppermute | solution.py:358
  32.1 20.8 %collective-permute-start.3 = (bf16[8,192,256]{2,1,0:T(8,128)(2,1)S(1)}, bf16[8,192,256]{2,1,0:T(8,128)(2,1)S(1)}, u32[]{:S(2)}, u32[]{:S(2)}) collective-permute-start(bf16[8,192,256]{2,1,0:T(8,128)(2,1)S(1)} %fusion), channel_id=1, source_target_pairs={{0,2},{1,3},{2,0},{3,1},{4,6},{5,7},{6,4},{7,5},{8,10},{9,11},{10,... | collective-permute-start | bytes 2359304 | tf_op jit(solution)/shard_map/ppermute | solution.py:364
  57.5 25.2 %collective-permute-start.5 = (bf16[2,8,192,256]{3,2,1,0:T(8,128)(2,1)S(1)}, bf16[2,8,192,256]{3,2,1,0:T(8,128)(2,1)S(1)}, u32[]{:S(2)}, u32[]{:S(2)}) collective-permute-start(bf16[2,8,192,256]{3,2,1,0:T(8,128)(2,1)S(1)} %shard_map.107), channel_id=1, source_target_pairs={{0,1},{1,0},{2,3},{3,2},{4,5},{5,4},{6,7},{7,6},{8,9},{9,8},{10,11... | collective-permute-start | bytes 4718600 | tf_op jit(solution)/shard_map/ppermute | solution.py:358
  57.6 20.5 %collective-permute-start.4 = (bf16[8,192,256]{2,1,0:T(8,128)(2,1)S(1)}, bf16[8,192,256]{2,1,0:T(8,128)(2,1)S(1)}, u32[]{:S(2)}, u32[]{:S(2)}) collective-permute-start(bf16[8,192,256]{2,1,0:T(8,128)(2,1)S(1)} %fusion.1), channel_id=1, source_target_pairs={{0,2},{1,3},{2,0},{3,1},{4,6},{5,7},{6,4},{7,5},{8,10},{9,11},{10,... | collective-permute-start | bytes 2359304 | tf_op jit(solution)/shard_map/ppermute | solution.py:364
  59.4 50.9 %collective-permute-start.6 = (bf16[8,192,256]{2,1,0:T(8,128)(2,1)S(1)}, bf16[8,192,256]{2,1,0:T(8,128)(2,1)S(1)}, u32[]{:S(2)}, u32[]{:S(2)}) collective-permute-start(bf16[8,192,256]{2,1,0:T(8,128)(2,1)S(1)} %fusion.2), channel_id=1, source_target_pairs={{0,2},{1,3},{2,0},{3,1},{4,6},{5,7},{6,4},{7,5},{8,10},{9,11},{10,... | collective-permute-start | bytes 2359304 | tf_op jit(solution)/shard_map/ppermute | solution.py:364
  83.0 46.2 %collective-permute-start.7 = (bf16[8,192,256]{2,1,0:T(8,128)(2,1)S(1)}, bf16[8,192,256]{2,1,0:T(8,128)(2,1)S(1)}, u32[]{:S(2)}, u32[]{:S(2)}) collective-permute-start(bf16[8,192,256]{2,1,0:T(8,128)(2,1)S(1)} %fusion.3), channel_id=1, source_target_pairs={{0,2},{1,3},{2,0},{3,1},{4,6},{5,7},{6,4},{7,5},{8,10},{9,11},{10,... | collective-permute-start | bytes 2359304 | tf_op jit(solution)/shard_map/ppermute | solution.py:364
  84.8 4.7 %collective-permute-start.8 = (bf16[192,256]{1,0:T(8,128)(2,1)S(1)}, bf16[192,256]{1,0:T(8,128)(2,1)S(1)}, u32[]{:S(2)}, u32[]{:S(2)}) collective-permute-start(bf16[192,256]{1,0:T(8,128)(2,1)S(1)} %get-tuple-element.82), channel_id=1, source_target_pairs={{0,4},{4,0},{8,12},{12,8},{16,20},{20,16},{24,28},{28,24},{1,5},{5... | collective-permute-start | bytes 294920 | tf_op jit(solution)/shard_map/ppermute | solution.py:374
  86.3 5.8 %collective-permute-start.9 = (bf16[192,256]{1,0:T(8,128)(2,1)S(1)}, bf16[192,256]{1,0:T(8,128)(2,1)S(1)}, u32[]{:S(2)}, u32[]{:S(2)}) collective-permute-start(bf16[192,256]{1,0:T(8,128)(2,1)S(1)} %get-tuple-element.83), channel_id=1, source_target_pairs={{0,8},{4,12},{8,0},{12,4},{16,24},{20,28},{24,16},{28,20},{1,9},{5... | collective-permute-start | bytes 294920 | tf_op jit(solution)/shard_map/ppermute | solution.py:374
  87.9 6.7 %collective-permute-start.10 = (bf16[192,256]{1,0:T(8,128)(2,1)S(1)}, bf16[192,256]{1,0:T(8,128)(2,1)S(1)}, u32[]{:S(2)}, u32[]{:S(2)}) collective-permute-start(bf16[192,256]{1,0:T(8,128)(2,1)S(1)} %get-tuple-element.84), channel_id=1, source_target_pairs={{0,12},{4,8},{8,4},{12,0},{16,28},{20,24},{24,20},{28,16},{1,13},{... | collective-permute-start | bytes 294920 | tf_op jit(solution)/shard_map/ppermute | solution.py:374
  89.5 12.8 %collective-permute-start.11 = (bf16[192,256]{1,0:T(8,128)(2,1)S(1)}, bf16[192,256]{1,0:T(8,128)(2,1)S(1)}, u32[]{:S(2)}, u32[]{:S(2)}) collective-permute-start(bf16[192,256]{1,0:T(8,128)(2,1)S(1)} %get-tuple-element.85), channel_id=1, source_target_pairs={{0,16},{4,20},{8,24},{12,28},{16,0},{20,4},{24,8},{28,12},{1,17},{... | collective-permute-start | bytes 294920 | tf_op jit(solution)/shard_map/ppermute | solution.py:374
  92.1 14.0 %collective-permute-start.12 = (bf16[192,256]{1,0:T(8,128)(2,1)S(1)}, bf16[192,256]{1,0:T(8,128)(2,1)S(1)}, u32[]{:S(2)}, u32[]{:S(2)}) collective-permute-start(bf16[192,256]{1,0:T(8,128)(2,1)S(1)} %get-tuple-element.86), channel_id=1, source_target_pairs={{0,20},{4,16},{8,28},{12,24},{16,4},{20,0},{24,12},{28,8},{1,21},{... | collective-permute-start | bytes 294920 | tf_op jit(solution)/shard_map/ppermute | solution.py:374
  94.5 11.8 %collective-permute-start.13 = (bf16[192,256]{1,0:T(8,128)(2,1)S(1)}, bf16[192,256]{1,0:T(8,128)(2,1)S(1)}, u32[]{:S(2)}, u32[]{:S(2)}) collective-permute-start(bf16[192,256]{1,0:T(8,128)(2,1)S(1)} %get-tuple-element.87), channel_id=1, source_target_pairs={{0,24},{4,28},{8,16},{12,20},{16,8},{20,12},{24,0},{28,4},{1,25},{... | collective-permute-start | bytes 294920 | tf_op jit(solution)/shard_map/ppermute | solution.py:374
  102.3 8.0 %collective-permute-start.14 = (bf16[192,256]{1,0:T(8,128)(2,1)S(1)}, bf16[192,256]{1,0:T(8,128)(2,1)S(1)}, u32[]{:S(2)}, u32[]{:S(2)}) collective-permute-start(bf16[192,256]{1,0:T(8,128)(2,1)S(1)} %get-tuple-element.88), channel_id=1, source_target_pairs={{0,28},{4,24},{8,20},{12,16},{16,12},{20,8},{24,4},{28,0},{1,29},{... | collective-permute-start | bytes 294920 | tf_op jit(solution)/shard_map/ppermute | solution.py:374
  106.1 8.1 %collective-permute-start.15 = (bf16[192,256]{1,0:T(8,128)(2,1)S(1)}, bf16[192,256]{1,0:T(8,128)(2,1)S(1)}, u32[]{:S(2)}, u32[]{:S(2)}) collective-permute-start(bf16[192,256]{1,0:T(8,128)(2,1)S(1)} %get-tuple-element.89), channel_id=1, source_target_pairs={{0,4},{4,0},{8,12},{12,8},{16,20},{20,16},{24,28},{28,24},{1,5},{5... | collective-permute-start | bytes 294920 | tf_op jit(solution)/shard_map/ppermute | solution.py:374
  106.4 7.8 %collective-permute-start.16 = (bf16[192,256]{1,0:T(8,128)(2,1)S(1)}, bf16[192,256]{1,0:T(8,128)(2,1)S(1)}, u32[]{:S(2)}, u32[]{:S(2)}) collective-permute-start(bf16[192,256]{1,0:T(8,128)(2,1)S(1)} %get-tuple-element.90), channel_id=1, source_target_pairs={{0,8},{4,12},{8,0},{12,4},{16,24},{20,28},{24,16},{28,20},{1,9},{5... | collective-permute-start | bytes 294920 | tf_op jit(solution)/shard_map/ppermute | solution.py:374
  110.3 7.2 %collective-permute-start.17 = (bf16[192,256]{1,0:T(8,128)(2,1)S(1)}, bf16[192,256]{1,0:T(8,128)(2,1)S(1)}, u32[]{:S(2)}, u32[]{:S(2)}) collective-permute-start(bf16[192,256]{1,0:T(8,128)(2,1)S(1)} %get-tuple-element.91), channel_id=1, source_target_pairs={{0,12},{4,8},{8,4},{12,0},{16,28},{20,24},{24,20},{28,16},{1,13},{... | collective-permute-start | bytes 294920 | tf_op jit(solution)/shard_map/ppermute | solution.py:374
  110.3 13.5 %collective-permute-start.18 = (bf16[192,256]{1,0:T(8,128)(2,1)S(1)}, bf16[192,256]{1,0:T(8,128)(2,1)S(1)}, u32[]{:S(2)}, u32[]{:S(2)}) collective-permute-start(bf16[192,256]{1,0:T(8,128)(2,1)S(1)} %get-tuple-element.92), channel_id=1, source_target_pairs={{0,16},{4,20},{8,24},{12,28},{16,0},{20,4},{24,8},{28,12},{1,17},{... | collective-permute-start | bytes 294920 | tf_op jit(solution)/shard_map/ppermute | solution.py:374
  114.2 12.4 %collective-permute-start.19 = (bf16[192,256]{1,0:T(8,128)(2,1)S(1)}, bf16[192,256]{1,0:T(8,128)(2,1)S(1)}, u32[]{:S(2)}, u32[]{:S(2)}) collective-permute-start(bf16[192,256]{1,0:T(8,128)(2,1)S(1)} %get-tuple-element.93), channel_id=1, source_target_pairs={{0,20},{4,16},{8,28},{12,24},{16,4},{20,0},{24,12},{28,8},{1,21},{... | collective-permute-start | bytes 294920 | tf_op jit(solution)/shard_map/ppermute | solution.py:374
  114.2 15.7 %copy-start.2 = (f32[4,48,384]{2,1,0:T(8,128)S(1)}, f32[4,48,384]{2,1,0:T(8,128)}, u32[]{:S(2)}) copy-start(f32[4,48,384]{2,1,0:T(8,128)} %constant.20.clone.vs_ref) | copy-start | bytes 884740
  114.2 15.7 %copy-start.3 = (f32[4,48,384]{2,1,0:T(8,128)S(1)}, f32[4,48,384]{2,1,0:T(8,128)}, u32[]{:S(2)}) copy-start(f32[4,48,384]{2,1,0:T(8,128)} %constant.19.clone.vc_ref) | copy-start | bytes 884740
  114.2 15.7 %copy-start.5 = (f32[8,384]{1,0:T(8,128)S(1)}, f32[8,384]{1,0:T(8,128)}, u32[]{:S(2)}) copy-start(f32[8,384]{1,0:T(8,128)} %constant.17.clone.uc_ref) | copy-start | bytes 36868
  114.2 15.7 %copy-start.6 = (f32[8,384]{1,0:T(8,128)S(1)}, f32[8,384]{1,0:T(8,128)}, u32[]{:S(2)}) copy-start(f32[8,384]{1,0:T(8,128)} %constant.18.clone.us_ref) | copy-start | bytes 36868
  114.2 12.3 %collective-permute-start.20 = (bf16[192,256]{1,0:T(8,128)(2,1)S(1)}, bf16[192,256]{1,0:T(8,128)(2,1)S(1)}, u32[]{:S(2)}, u32[]{:S(2)}) collective-permute-start(bf16[192,256]{1,0:T(8,128)(2,1)S(1)} %get-tuple-element.94), channel_id=1, source_target_pairs={{0,24},{4,28},{8,16},{12,20},{16,8},{20,12},{24,0},{28,4},{1,25},{... | collective-permute-start | bytes 294920 | tf_op jit(solution)/shard_map/ppermute | solution.py:374
  117.5 14.3 %collective-permute-start.21 = (bf16[192,256]{1,0:T(8,128)(2,1)S(1)}, bf16[192,256]{1,0:T(8,128)(2,1)S(1)}, u32[]{:S(2)}, u32[]{:S(2)}) collective-permute-start(bf16[192,256]{1,0:T(8,128)(2,1)S(1)} %get-tuple-element.95), channel_id=1, source_target_pairs={{0,28},{4,24},{8,20},{12,16},{16,12},{20,8},{24,4},{28,0},{1,29},{... | collective-permute-start | bytes 294920 | tf_op jit(solution)/shard_map/ppermute | solution.py:374
  123.8 11.4 %collective-permute-start.22 = (bf16[192,256]{1,0:T(8,128)(2,1)S(1)}, bf16[192,256]{1,0:T(8,128)(2,1)S(1)}, u32[]{:S(2)}, u32[]{:S(2)}) collective-permute-start(bf16[192,256]{1,0:T(8,128)(2,1)S(1)} %get-tuple-element.98), channel_id=1, source_target_pairs={{0,4},{4,0},{8,12},{12,8},{16,20},{20,16},{24,28},{28,24},{1,5},{5... | collective-permute-start | bytes 294920 | tf_op jit(solution)/shard_map/ppermute | solution.py:374
  126.5 10.6 %collective-permute-start.23 = (bf16[192,256]{1,0:T(8,128)(2,1)S(1)}, bf16[192,256]{1,0:T(8,128)(2,1)S(1)}, u32[]{:S(2)}, u32[]{:S(2)}) collective-permute-start(bf16[192,256]{1,0:T(8,128)(2,1)S(1)} %get-tuple-element.99), channel_id=1, source_target_pairs={{0,8},{4,12},{8,0},{12,4},{16,24},{20,28},{24,16},{28,20},{1,9},{5... | collective-permute-start | bytes 294920 | tf_op jit(solution)/shard_map/ppermute | solution.py:374
  126.5 12.2 %collective-permute-start.24 = (bf16[192,256]{1,0:T(8,128)(2,1)S(1)}, bf16[192,256]{1,0:T(8,128)(2,1)S(1)}, u32[]{:S(2)}, u32[]{:S(2)}) collective-permute-start(bf16[192,256]{1,0:T(8,128)(2,1)S(1)} %get-tuple-element.100), channel_id=1, source_target_pairs={{0,12},{4,8},{8,4},{12,0},{16,28},{20,24},{24,20},{28,16},{1,13},{... | collective-permute-start | bytes 294920 | tf_op jit(solution)/shard_map/ppermute | solution.py:374
  129.2 11.3 %collective-permute-start.25 = (bf16[192,256]{1,0:T(8,128)(2,1)S(1)}, bf16[192,256]{1,0:T(8,128)(2,1)S(1)}, u32[]{:S(2)}, u32[]{:S(2)}) collective-permute-start(bf16[192,256]{1,0:T(8,128)(2,1)S(1)} %get-tuple-element.101), channel_id=1, source_target_pairs={{0,16},{4,20},{8,24},{12,28},{16,0},{20,4},{24,8},{28,12},{1,17},{... | collective-permute-start | bytes 294920 | tf_op jit(solution)/shard_map/ppermute | solution.py:374
  131.8 14.4 %collective-permute-start.26 = (bf16[192,256]{1,0:T(8,128)(2,1)S(1)}, bf16[192,256]{1,0:T(8,128)(2,1)S(1)}, u32[]{:S(2)}, u32[]{:S(2)}) collective-permute-start(bf16[192,256]{1,0:T(8,128)(2,1)S(1)} %get-tuple-element.102), channel_id=1, source_target_pairs={{0,20},{4,16},{8,28},{12,24},{16,4},{20,0},{24,12},{28,8},{1,21},{... | collective-permute-start | bytes 294920 | tf_op jit(solution)/shard_map/ppermute | solution.py:374
  135.2 11.0 %collective-permute-start.27 = (bf16[192,256]{1,0:T(8,128)(2,1)S(1)}, bf16[192,256]{1,0:T(8,128)(2,1)S(1)}, u32[]{:S(2)}, u32[]{:S(2)}) collective-permute-start(bf16[192,256]{1,0:T(8,128)(2,1)S(1)} %get-tuple-element.103), channel_id=1, source_target_pairs={{0,24},{4,28},{8,16},{12,20},{16,8},{20,12},{24,0},{28,4},{1,25},{... | collective-permute-start | bytes 294920 | tf_op jit(solution)/shard_map/ppermute | solution.py:374
  137.1 14.6 %collective-permute-start.28 = (bf16[192,256]{1,0:T(8,128)(2,1)S(1)}, bf16[192,256]{1,0:T(8,128)(2,1)S(1)}, u32[]{:S(2)}, u32[]{:S(2)}) collective-permute-start(bf16[192,256]{1,0:T(8,128)(2,1)S(1)} %get-tuple-element.104), channel_id=1, source_target_pairs={{0,28},{4,24},{8,20},{12,16},{16,12},{20,8},{24,4},{28,0},{1,29},{... | collective-permute-start | bytes 294920 | tf_op jit(solution)/shard_map/ppermute | solution.py:374
  138.8 15.9 %collective-permute-start.29 = (bf16[192,256]{1,0:T(8,128)(2,1)S(1)}, bf16[192,256]{1,0:T(8,128)(2,1)S(1)}, u32[]{:S(2)}, u32[]{:S(2)}) collective-permute-start(bf16[192,256]{1,0:T(8,128)(2,1)S(1)} %get-tuple-element.106), channel_id=1, source_target_pairs={{0,4},{4,0},{8,12},{12,8},{16,20},{20,16},{24,28},{28,24},{1,5},{5... | collective-permute-start | bytes 294920 | tf_op jit(solution)/shard_map/ppermute | solution.py:374
  140.5 15.6 %collective-permute-start.30 = (bf16[192,256]{1,0:T(8,128)(2,1)S(1)}, bf16[192,256]{1,0:T(8,128)(2,1)S(1)}, u32[]{:S(2)}, u32[]{:S(2)}) collective-permute-start(bf16[192,256]{1,0:T(8,128)(2,1)S(1)} %get-tuple-element.107), channel_id=1, source_target_pairs={{0,8},{4,12},{8,0},{12,4},{16,24},{20,28},{24,16},{28,20},{1,9},{5... | collective-permute-start | bytes 294920 | tf_op jit(solution)/shard_map/ppermute | solution.py:374
  146.1 20.2 %collective-permute-start.31 = (bf16[192,256]{1,0:T(8,128)(2,1)S(1)}, bf16[192,256]{1,0:T(8,128)(2,1)S(1)}, u32[]{:S(2)}, u32[]{:S(2)}) collective-permute-start(bf16[192,256]{1,0:T(8,128)(2,1)S(1)} %get-tuple-element.108), channel_id=1, source_target_pairs={{0,12},{4,8},{8,4},{12,0},{16,28},{20,24},{24,20},{28,16},{1,13},{... | collective-permute-start | bytes 294920 | tf_op jit(solution)/shard_map/ppermute | solution.py:374
  146.1 20.2 %collective-permute-start.32 = (bf16[192,256]{1,0:T(8,128)(2,1)S(1)}, bf16[192,256]{1,0:T(8,128)(2,1)S(1)}, u32[]{:S(2)}, u32[]{:S(2)}) collective-permute-start(bf16[192,256]{1,0:T(8,128)(2,1)S(1)} %get-tuple-element.109), channel_id=1, source_target_pairs={{0,16},{4,20},{8,24},{12,28},{16,0},{20,4},{24,8},{28,12},{1,17},{... | collective-permute-start | bytes 294920 | tf_op jit(solution)/shard_map/ppermute | solution.py:374
  151.7 14.6 %collective-permute-start.33 = (bf16[192,256]{1,0:T(8,128)(2,1)S(1)}, bf16[192,256]{1,0:T(8,128)(2,1)S(1)}, u32[]{:S(2)}, u32[]{:S(2)}) collective-permute-start(bf16[192,256]{1,0:T(8,128)(2,1)S(1)} %get-tuple-element.110), channel_id=1, source_target_pairs={{0,20},{4,16},{8,28},{12,24},{16,4},{20,0},{24,12},{28,8},{1,21},{... | collective-permute-start | bytes 294920 | tf_op jit(solution)/shard_map/ppermute | solution.py:374
  154.7 11.6 %collective-permute-start.34 = (bf16[192,256]{1,0:T(8,128)(2,1)S(1)}, bf16[192,256]{1,0:T(8,128)(2,1)S(1)}, u32[]{:S(2)}, u32[]{:S(2)}) collective-permute-start(bf16[192,256]{1,0:T(8,128)(2,1)S(1)} %get-tuple-element.111), channel_id=1, source_target_pairs={{0,24},{4,28},{8,16},{12,20},{16,8},{20,12},{24,0},{28,4},{1,25},{... | collective-permute-start | bytes 294920 | tf_op jit(solution)/shard_map/ppermute | solution.py:374
  156.1 2.9 %copy-start.4 = (s32[2,1536]{1,0:T(2,128)S(1)}, s32[2,1536]{1,0:T(2,128)}, u32[]{:S(2)}) copy-start(s32[2,1536]{1,0:T(2,128)} %refs_10_.1) | copy-start | bytes 36868
  156.1 10.2 %collective-permute-start.35 = (bf16[192,256]{1,0:T(8,128)(2,1)S(1)}, bf16[192,256]{1,0:T(8,128)(2,1)S(1)}, u32[]{:S(2)}, u32[]{:S(2)}) collective-permute-start(bf16[192,256]{1,0:T(8,128)(2,1)S(1)} %get-tuple-element.112), channel_id=1, source_target_pairs={{0,28},{4,24},{8,20},{12,16},{16,12},{20,8},{24,4},{28,0},{1,29},{... | collective-permute-start | bytes 294920 | tf_op jit(solution)/shard_map/ppermute | solution.py:374
  (1 other events, 2.2 us)
where the time goes:
time: 170 us
  starting transfers between devices  59.9 us (35%)
  waiting for transfers between devices  51.6 us (30%)
  Pallas kernels  46.1 us (27%)
  local copies, waits for them, and re-layouts  10.5 us (6%)
  other arithmetic  1.73 us (1%)
    ppermute x28, starting transfers between devices, local(): lax.ppermute(total[i][r], 'chan', xor_pairs(n_chan, r))  51.7 us
    ppermute x4, waiting for transfers between devices, local(): far[i] = lax.ppermute(sent[i], 'bl', xor_pairs(n_bl, 2))  31.9 us
    pallas_call x8, Pallas kernels, grid_call(): pl.pallas_call(functools.partial(grid_kernel, inner, owned, n_bl, 2 * off...  30.7 us
    ppermute x28, waiting for transfers between devices, local(): lax.ppermute(total[i][r], 'chan', xor_pairs(n_chan, r))  19.7 us
    pallas_call x3, Pallas kernels, turn_call(): pl.pallas_call(functools.partial(turn_kernel, [len(g) for g in gs], has_a...  11.1 us
    unnamed x26, local copies, waits for them, and re-layouts  10.5 us
    ppermute x4, starting transfers between devices, local(): far[i] = lax.ppermute(sent[i], 'bl', xor_pairs(n_bl, 2))  6.89 us
  transfers between devices with their start and end apart: 36, of which 8 were waited for; matrix products, arithmetic and copies ran while one was open for 0% of the time, Pallas kernels for 18%

commit v1 on v0

--- a/solution.py
+++ b/solution.py
@@ -13,7 +13,7 @@
 UNIT = 16
 SHARES = (1, 1)
 DIRECT = (True, True, True, True)
-PER = 2
+PER = 8
 RADIX = 4
 LANES = 128
 
@@ -370,9 +370,9 @@
                 gate = total[i] = sum_all(after(keep[i], gate)[1], near[i][1], far[i])
         elif what == "spread":
             if DIRECT[i % len(DIRECT)]:
-                arrived[blocks[i]] = [total[i][0]] + [
-                    lax.ppermute(total[i][r], "chan", xor_pairs(n_chan, r)) for r in range(1, n_chan)
-                ]
+                arrived[blocks[i]] = list(total[i])
+                for r in range(1, n_chan):
+                    arrived[blocks[i]][r] = lax.ppermute(total[i][r], "chan", xor_pairs(n_chan, r))
             else:
                 arrived[blocks[i]] = [lax.all_to_all(total[i], "chan", 0, 0, tiled=True)]
         elif what == "join":

time: 170 us -> 164 us (0.965)
  Pallas kernels: 46.1 us -> 37.5 us
  local copies, waits for them, and re-layouts: 10.5 us -> 12.3 us
    pallas_call x8, Pallas kernels: 30.7 us -> 21.8 us  [grid_call(): pl.pallas_call(functools.partial(grid_kernel, inner, owned, n_bl, 2 * off...]
    unnamed x26, local copies, waits for them, and re-layouts: 10.5 us -> 12.2 us
  transfers between devices with their start and end apart: 36 -> 36, of which waited for: 8 -> 9; matrix products, arithmetic and copies ran while one was open for 0% -> 0% of each run, Pallas kernels for 18% -> 15%
where the time goes in v1:
time: 164 us; the launch traced here: 163 us
  starting transfers between devices  58.8 us (36%)
  waiting for transfers between devices  52.6 us (32%)
  Pallas kernels  37.5 us (23%)
  local copies, waits for them, and re-layouts  12.3 us (8%)
  other arithmetic  1.73 us (1%)
    ppermute x28, starting transfers between devices, local(): lax.ppermute(total[i][r], 'chan', xor_pairs(n_chan, r))  50.7 us
    ppermute x4, waiting for transfers between devices, local(): far[i] = lax.ppermute(sent[i], 'bl', xor_pairs(n_bl, 2))  33 us
    pallas_call x8, Pallas kernels, grid_call(): pl.pallas_call(functools.partial(grid_kernel, inner, owned, n_bl, 2 * off...  21.8 us
    ppermute x28, waiting for transfers between devices, local(): lax.ppermute(total[i][r], 'chan', xor_pairs(n_chan, r))  19.3 us
    unnamed x26, local copies, waits for them, and re-layouts  12.2 us
    pallas_call x3, Pallas kernels, turn_call(): pl.pallas_call(functools.partial(turn_kernel, [len(g) for g in gs], has_a...  11.1 us
    ppermute x4, starting transfers between devices, local(): far[i] = lax.ppermute(sent[i], 'bl', xor_pairs(n_bl, 2))  6.91 us
    pallas_call x4, Pallas kernels, sum_call(): pl.pallas_call(sum_kernel, grid_spec=pltpu.PrefetchScalarGridSpec(num_sca...  3.31 us
  transfers between devices with their start and end apart: 36, of which 9 were waited for; matrix products, arithmetic and copies ran while one was open for 0% of the time, Pallas kernels for 15%

profile of v1, /device:TPU:0, one launch (start us, length us, event | category | flops | bytes accessed | tf_op | source)
XLA Modules:
  0.0 163.4 jit_solution(11656012395587715830)
XLA Ops:
  0.1 0.8 add_add_fusion.lists_ref
  0.9 8.2 %copy-done = bf16[256,192,2,128]{3,2,1,0:T(2,128)(2,1)S(1)} copy-done((bf16[256,192,2,128]{3,2,1,0:T(2,128)(2,1)S(1)}, bf16[256,192,2,128]{3,2,1,0:T(2,128)(2,1)}, u32[]{:S(2)}) %copy-start) | copy-done | bytes 25165848
  9.1 2.2 %copy-done.1 = bf16[64,128,256]{2,1,0:T(8,128)(2,1)S(1)} copy-done((bf16[64,128,256]{2,1,0:T(8,128)(2,1)S(1)}, bf16[64,128,256]{2,1,0:T(8,128)(2,1)}, u32[]{:S(2)}) %copy-start.1) | copy-done | bytes 4194328
  11.3 2.7 %shard_map.100 = bf16[2,8,192,256]{3,2,1,0:T(8,128)(2,1)S(1)} custom-call(s32[18,64]{1,0:T(8,128)S(1)} %add_add_fusion.lists_ref, bf16[256,384,128]{2,1,0:T(8,128)(2,1)S(1)} %bitcast.18, bf16[64,128,256]{2,1,0:T(8,128)(2,1)S(1)} %copy-done.1), custom_call_target="tpu_custom_call" | custom-call | tf_op jit(solution)/shard_map/pallas_call | solution.py:62
  14.6 2.7 %shard_map.101.keep_ref = bf16[2,8,192,256]{3,2,1,0:T(8,128)(2,1)S(1)} custom-call(s32[18,64]{1,0:T(8,128)S(1)} %add_add_fusion.lists_ref, bf16[256,384,128]{2,1,0:T(8,128)(2,1)S(1)} %bitcast.19, bf16[64,128,256]{2,1,0:T(8,128)(2,1)S(1)} %copy-done.1), custom_call_target="tpu_custom_call" | custom-call | tf_op jit(solution)/shard_map/pallas_call | solution.py:62
  18.6 1.2 slice-done.5
  19.8 2.7 %shard_map.102 = bf16[2,8,192,256]{3,2,1,0:T(8,128)(2,1)S(1)} custom-call(s32[18,64]{1,0:T(8,128)S(1)} %add_add_fusion.lists_ref, bf16[256,384,128]{2,1,0:T(8,128)(2,1)S(1)} %bitcast.22, bf16[64,128,256]{2,1,0:T(8,128)(2,1)S(1)} %copy-done.1), custom_call_target="tpu_custom_call" | custom-call | tf_op jit(solution)/shard_map/pallas_call | solution.py:62
  23.1 2.7 %shard_map.103.keep_ref = bf16[2,8,192,256]{3,2,1,0:T(8,128)(2,1)S(1)} custom-call(s32[18,64]{1,0:T(8,128)S(1)} %add_add_fusion.lists_ref, bf16[256,384,128]{2,1,0:T(8,128)(2,1)S(1)} %bitcast.23, bf16[64,128,256]{2,1,0:T(8,128)(2,1)S(1)} %copy-done.1), custom_call_target="tpu_custom_call" | custom-call | tf_op jit(solution)/shard_map/pallas_call | solution.py:62
  25.8 2.7 %shard_map.104 = bf16[2,8,192,256]{3,2,1,0:T(8,128)(2,1)S(1)} custom-call(s32[18,64]{1,0:T(8,128)S(1)} %add_add_fusion.lists_ref, bf16[256,384,128]{2,1,0:T(8,128)(2,1)S(1)} %bitcast.24, bf16[64,128,256]{2,1,0:T(8,128)(2,1)S(1)} %copy-done.1), custom_call_target="tpu_custom_call" | custom-call | tf_op jit(solution)/shard_map/pallas_call | solution.py:62
  28.6 3.0 %collective-permute-start.3 = (bf16[8,192,256]{2,1,0:T(8,128)(2,1)S(1)}, bf16[8,192,256]{2,1,0:T(8,128)(2,1)S(1)}, u32[]{:S(2)}, u32[]{:S(2)}) collective-permute-start(bf16[8,192,256]{2,1,0:T(8,128)(2,1)S(1)} %fusion), channel_id=1, source_target_pairs={{0,2},{1,3},{2,0},{3,1},{4,6},{5,7},{6,4},{7,5},{8,10},{9,11},{10,... | collective-permute-start | bytes 2359304 | tf_op jit(solution)/shard_map/ppermute | solution.py:364
  31.8 2.7 %shard_map.105.keep_ref = bf16[2,8,192,256]{3,2,1,0:T(8,128)(2,1)S(1)} custom-call(s32[18,64]{1,0:T(8,128)S(1)} %add_add_fusion.lists_ref, bf16[256,384,128]{2,1,0:T(8,128)(2,1)S(1)} %bitcast.25, bf16[64,128,256]{2,1,0:T(8,128)(2,1)S(1)} %copy-done.1), custom_call_target="tpu_custom_call" | custom-call | tf_op jit(solution)/shard_map/pallas_call | solution.py:62
  34.8 14.6 %collective-permute-done.3.far_ref = bf16[8,192,256]{2,1,0:T(8,128)(2,1)S(1)} collective-permute-done((bf16[8,192,256]{2,1,0:T(8,128)(2,1)S(1)}, bf16[8,192,256]{2,1,0:T(8,128)(2,1)S(1)}, u32[]{:S(2)}, u32[]{:S(2)}) %collective-permute-start.3) | collective-permute-done | bytes 786464 | tf_op jit(solution)/shard_map/ppermute | solution.py:364
  49.4 0.8 shard_map.106
  50.2 2.7 %shard_map.107 = bf16[2,8,192,256]{3,2,1,0:T(8,128)(2,1)S(1)} custom-call(s32[18,64]{1,0:T(8,128)S(1)} %add_add_fusion.lists_ref, bf16[256,384,128]{2,1,0:T(8,128)(2,1)S(1)} %bitcast.26, bf16[64,128,256]{2,1,0:T(8,128)(2,1)S(1)} %copy-done.1), custom_call_target="tpu_custom_call" | custom-call | tf_op jit(solution)/shard_map/pallas_call | solution.py:62
  53.0 1.8 %collective-permute-start.4 = (bf16[8,192,256]{2,1,0:T(8,128)(2,1)S(1)}, bf16[8,192,256]{2,1,0:T(8,128)(2,1)S(1)}, u32[]{:S(2)}, u32[]{:S(2)}) collective-permute-start(bf16[8,192,256]{2,1,0:T(8,128)(2,1)S(1)} %fusion.1), channel_id=1, source_target_pairs={{0,2},{1,3},{2,0},{3,1},{4,6},{5,7},{6,4},{7,5},{8,10},{9,11},{10,... | collective-permute-start | bytes 2359304 | tf_op jit(solution)/shard_map/ppermute | solution.py:364
  55.1 18.4 %collective-permute-done.4.far_ref = bf16[8,192,256]{2,1,0:T(8,128)(2,1)S(1)} collective-permute-done((bf16[8,192,256]{2,1,0:T(8,128)(2,1)S(1)}, bf16[8,192,256]{2,1,0:T(8,128)(2,1)S(1)}, u32[]{:S(2)}, u32[]{:S(2)}) %collective-permute-start.4) | collective-permute-done | bytes 786464 | tf_op jit(solution)/shard_map/ppermute | solution.py:364
  73.5 0.8 shard_map.108
  74.4 2.7 %shard_map.109.keep_ref = bf16[2,8,192,256]{3,2,1,0:T(8,128)(2,1)S(1)} custom-call(s32[18,64]{1,0:T(8,128)S(1)} %add_add_fusion.lists_ref, bf16[256,384,128]{2,1,0:T(8,128)(2,1)S(1)} %bitcast.27, bf16[64,128,256]{2,1,0:T(8,128)(2,1)S(1)} %copy-done.1), custom_call_target="tpu_custom_call" | custom-call | tf_op jit(solution)/shard_map/pallas_call | solution.py:62
  77.3 1.8 %collective-permute-start.7 = (bf16[8,192,256]{2,1,0:T(8,128)(2,1)S(1)}, bf16[8,192,256]{2,1,0:T(8,128)(2,1)S(1)}, u32[]{:S(2)}, u32[]{:S(2)}) collective-permute-start(bf16[8,192,256]{2,1,0:T(8,128)(2,1)S(1)} %fusion.3), channel_id=1, source_target_pairs={{0,2},{1,3},{2,0},{3,1},{4,6},{5,7},{6,4},{7,5},{8,10},{9,11},{10,... | collective-permute-start | bytes 2359304 | tf_op jit(solution)/shard_map/ppermute | solution.py:364
  79.1 1.5 collective-permute-start.8
  80.6 1.6 collective-permute-start.9
  82.6 1.2 collective-permute-done.8.refs_1_
  83.8 2.6 %collective-permute-start.11 = (bf16[192,256]{1,0:T(8,128)(2,1)S(1)}, bf16[192,256]{1,0:T(8,128)(2,1)S(1)}, u32[]{:S(2)}, u32[]{:S(2)}) collective-permute-start(bf16[192,256]{1,0:T(8,128)(2,1)S(1)} %get-tuple-element.85), channel_id=1, source_target_pairs={{0,16},{4,20},{8,24},{12,28},{16,0},{20,4},{24,8},{28,12},{1,17},{... | collective-permute-start | bytes 294920 | tf_op jit(solution)/shard_map/ppermute | solution.py:375
  86.4 2.4 %collective-permute-start.12 = (bf16[192,256]{1,0:T(8,128)(2,1)S(1)}, bf16[192,256]{1,0:T(8,128)(2,1)S(1)}, u32[]{:S(2)}, u32[]{:S(2)}) collective-permute-start(bf16[192,256]{1,0:T(8,128)(2,1)S(1)} %get-tuple-element.86), channel_id=1, source_target_pairs={{0,20},{4,16},{8,28},{12,24},{16,4},{20,0},{24,12},{28,8},{1,21},{... | collective-permute-start | bytes 294920 | tf_op jit(solution)/shard_map/ppermute | solution.py:375
  88.8 3.4 %collective-permute-start.13 = (bf16[192,256]{1,0:T(8,128)(2,1)S(1)}, bf16[192,256]{1,0:T(8,128)(2,1)S(1)}, u32[]{:S(2)}, u32[]{:S(2)}) collective-permute-start(bf16[192,256]{1,0:T(8,128)(2,1)S(1)} %get-tuple-element.87), channel_id=1, source_target_pairs={{0,24},{4,28},{8,16},{12,20},{16,8},{20,12},{24,0},{28,4},{1,25},{... | collective-permute-start | bytes 294920 | tf_op jit(solution)/shard_map/ppermute | solution.py:375
  92.3 4.3 %collective-permute-done.11.refs_4_ = bf16[192,256]{1,0:T(8,128)(2,1)S(1)} collective-permute-done((bf16[192,256]{1,0:T(8,128)(2,1)S(1)}, bf16[192,256]{1,0:T(8,128)(2,1)S(1)}, u32[]{:S(2)}, u32[]{:S(2)}) %collective-permute-start.11) | collective-permute-done | bytes 98336 | tf_op jit(solution)/shard_map/ppermute | solution.py:375
  96.6 3.8 %collective-permute-start.14 = (bf16[192,256]{1,0:T(8,128)(2,1)S(1)}, bf16[192,256]{1,0:T(8,128)(2,1)S(1)}, u32[]{:S(2)}, u32[]{:S(2)}) collective-permute-start(bf16[192,256]{1,0:T(8,128)(2,1)S(1)} %get-tuple-element.88), channel_id=1, source_target_pairs={{0,28},{4,24},{8,20},{12,16},{16,12},{20,8},{24,4},{28,0},{1,29},{... | collective-permute-start | bytes 294920 | tf_op jit(solution)/shard_map/ppermute | solution.py:375
  101.4 3.2 %collective-permute-done.14.refs_7_ = bf16[192,256]{1,0:T(8,128)(2,1)S(1)} collective-permute-done((bf16[192,256]{1,0:T(8,128)(2,1)S(1)}, bf16[192,256]{1,0:T(8,128)(2,1)S(1)}, u32[]{:S(2)}, u32[]{:S(2)}) %collective-permute-start.14) | collective-permute-done | bytes 98336 | tf_op jit(solution)/shard_map/ppermute | solution.py:375
  104.6 3.9 %collective-permute-start.18 = (bf16[192,256]{1,0:T(8,128)(2,1)S(1)}, bf16[192,256]{1,0:T(8,128)(2,1)S(1)}, u32[]{:S(2)}, u32[]{:S(2)}) collective-permute-start(bf16[192,256]{1,0:T(8,128)(2,1)S(1)} %get-tuple-element.92), channel_id=1, source_target_pairs={{0,16},{4,20},{8,24},{12,28},{16,0},{20,4},{24,8},{28,12},{1,17},{... | collective-permute-start | bytes 294920 | tf_op jit(solution)/shard_map/ppermute | solution.py:375
  108.6 2.4 %collective-permute-start.20 = (bf16[192,256]{1,0:T(8,128)(2,1)S(1)}, bf16[192,256]{1,0:T(8,128)(2,1)S(1)}, u32[]{:S(2)}, u32[]{:S(2)}) collective-permute-start(bf16[192,256]{1,0:T(8,128)(2,1)S(1)} %get-tuple-element.94), channel_id=1, source_target_pairs={{0,24},{4,28},{8,16},{12,20},{16,8},{20,12},{24,0},{28,4},{1,25},{... | collective-permute-start | bytes 294920 | tf_op jit(solution)/shard_map/ppermute | solution.py:375
  110.9 0.8 shard_map.110
  111.8 3.5 %collective-permute-start.21 = (bf16[192,256]{1,0:T(8,128)(2,1)S(1)}, bf16[192,256]{1,0:T(8,128)(2,1)S(1)}, u32[]{:S(2)}, u32[]{:S(2)}) collective-permute-start(bf16[192,256]{1,0:T(8,128)(2,1)S(1)} %get-tuple-element.95), channel_id=1, source_target_pairs={{0,28},{4,24},{8,20},{12,16},{16,12},{20,8},{24,4},{28,0},{1,29},{... | collective-permute-start | bytes 294920 | tf_op jit(solution)/shard_map/ppermute | solution.py:375
  115.3 2.7 %collective-permute-done.18.refs_12_ = bf16[192,256]{1,0:T(8,128)(2,1)S(1)} collective-permute-done((bf16[192,256]{1,0:T(8,128)(2,1)S(1)}, bf16[192,256]{1,0:T(8,128)(2,1)S(1)}, u32[]{:S(2)}, u32[]{:S(2)}) %collective-permute-start.18) | collective-permute-done | bytes 98336 | tf_op jit(solution)/shard_map/ppermute | solution.py:375
  118.4 2.4 %collective-permute-done.19.refs_13_ = bf16[192,256]{1,0:T(8,128)(2,1)S(1)} collective-permute-done((bf16[192,256]{1,0:T(8,128)(2,1)S(1)}, bf16[192,256]{1,0:T(8,128)(2,1)S(1)}, u32[]{:S(2)}, u32[]{:S(2)}) %collective-permute-start.19) | collective-permute-done | bytes 98336 | tf_op jit(solution)/shard_map/ppermute | solution.py:375
  120.9 2.6 %collective-permute-start.24 = (bf16[192,256]{1,0:T(8,128)(2,1)S(1)}, bf16[192,256]{1,0:T(8,128)(2,1)S(1)}, u32[]{:S(2)}, u32[]{:S(2)}) collective-permute-start(bf16[192,256]{1,0:T(8,128)(2,1)S(1)} %get-tuple-element.100), channel_id=1, source_target_pairs={{0,12},{4,8},{8,4},{12,0},{16,28},{20,24},{24,20},{28,16},{1,13},{... | collective-permute-start | bytes 294920 | tf_op jit(solution)/shard_map/ppermute | solution.py:375
  124.2 1.2 tables.1
  125.4 0.8 shard_map.111
  126.2 3.5 %collective-permute-start.26 = (bf16[192,256]{1,0:T(8,128)(2,1)S(1)}, bf16[192,256]{1,0:T(8,128)(2,1)S(1)}, u32[]{:S(2)}, u32[]{:S(2)}) collective-permute-start(bf16[192,256]{1,0:T(8,128)(2,1)S(1)} %get-tuple-element.102), channel_id=1, source_target_pairs={{0,20},{4,16},{8,28},{12,24},{16,4},{20,0},{24,12},{28,8},{1,21},{... | collective-permute-start | bytes 294920 | tf_op jit(solution)/shard_map/ppermute | solution.py:375
  129.7 1.9 %collective-permute-start.27 = (bf16[192,256]{1,0:T(8,128)(2,1)S(1)}, bf16[192,256]{1,0:T(8,128)(2,1)S(1)}, u32[]{:S(2)}, u32[]{:S(2)}) collective-permute-start(bf16[192,256]{1,0:T(8,128)(2,1)S(1)} %get-tuple-element.103), channel_id=1, source_target_pairs={{0,24},{4,28},{8,16},{12,20},{16,8},{20,12},{24,0},{28,4},{1,25},{... | collective-permute-start | bytes 294920 | tf_op jit(solution)/shard_map/ppermute | solution.py:375
  131.6 1.7 %collective-permute-start.28 = (bf16[192,256]{1,0:T(8,128)(2,1)S(1)}, bf16[192,256]{1,0:T(8,128)(2,1)S(1)}, u32[]{:S(2)}, u32[]{:S(2)}) collective-permute-start(bf16[192,256]{1,0:T(8,128)(2,1)S(1)} %get-tuple-element.104), channel_id=1, source_target_pairs={{0,28},{4,24},{8,20},{12,16},{16,12},{20,8},{24,4},{28,0},{1,29},{... | collective-permute-start | bytes 294920 | tf_op jit(solution)/shard_map/ppermute | solution.py:375
  133.3 1.7 %collective-permute-start.29 = (bf16[192,256]{1,0:T(8,128)(2,1)S(1)}, bf16[192,256]{1,0:T(8,128)(2,1)S(1)}, u32[]{:S(2)}, u32[]{:S(2)}) collective-permute-start(bf16[192,256]{1,0:T(8,128)(2,1)S(1)} %get-tuple-element.106), channel_id=1, source_target_pairs={{0,4},{4,0},{8,12},{12,8},{16,20},{20,16},{24,28},{28,24},{1,5},{5... | collective-permute-start | bytes 294920 | tf_op jit(solution)/shard_map/ppermute | solution.py:375
  135.0 5.4 %collective-permute-done.26.refs_5_ = bf16[192,256]{1,0:T(8,128)(2,1)S(1)} collective-permute-done((bf16[192,256]{1,0:T(8,128)(2,1)S(1)}, bf16[192,256]{1,0:T(8,128)(2,1)S(1)}, u32[]{:S(2)}, u32[]{:S(2)}) %collective-permute-start.26) | collective-permute-done | bytes 98336 | tf_op jit(solution)/shard_map/ppermute | solution.py:375
  140.4 3.0 %collective-permute-start.32 = (bf16[192,256]{1,0:T(8,128)(2,1)S(1)}, bf16[192,256]{1,0:T(8,128)(2,1)S(1)}, u32[]{:S(2)}, u32[]{:S(2)}) collective-permute-start(bf16[192,256]{1,0:T(8,128)(2,1)S(1)} %get-tuple-element.109), channel_id=1, source_target_pairs={{0,16},{4,20},{8,24},{12,28},{16,0},{20,4},{24,8},{28,12},{1,17},{... | collective-permute-start | bytes 294920 | tf_op jit(solution)/shard_map/ppermute | solution.py:375
  143.4 6.9 %collective-permute-start.33 = (bf16[192,256]{1,0:T(8,128)(2,1)S(1)}, bf16[192,256]{1,0:T(8,128)(2,1)S(1)}, u32[]{:S(2)}, u32[]{:S(2)}) collective-permute-start(bf16[192,256]{1,0:T(8,128)(2,1)S(1)} %get-tuple-element.110), channel_id=1, source_target_pairs={{0,20},{4,16},{8,28},{12,24},{16,4},{20,0},{24,12},{28,8},{1,21},{... | collective-permute-start | bytes 294920 | tf_op jit(solution)/shard_map/ppermute | solution.py:375
  150.4 1.6 %collective-permute-start.35 = (bf16[192,256]{1,0:T(8,128)(2,1)S(1)}, bf16[192,256]{1,0:T(8,128)(2,1)S(1)}, u32[]{:S(2)}, u32[]{:S(2)}) collective-permute-start(bf16[192,256]{1,0:T(8,128)(2,1)S(1)} %get-tuple-element.112), channel_id=1, source_target_pairs={{0,28},{4,24},{8,20},{12,16},{16,12},{20,8},{24,4},{28,0},{1,29},{... | collective-permute-start | bytes 294920 | tf_op jit(solution)/shard_map/ppermute | solution.py:375
  152.1 5.0 %shard_map.112.refs_11_ = f32[2,2,256,1536]{3,2,1,0:T(8,128)} custom-call(s32[2]{0:T(128)S(1)} %pad_add_fusion.me_ref, bf16[192,256]{1,0:T(8,128)(2,1)S(1)} %get-tuple-element.81.refs_0_, bf16[192,256]{1,0:T(8,128)(2,1)S(1)} %collective-permute-done.8.refs_1_, bf16[192,256]{1,0:T(8,128)(2,1)S(1)} %collective-permute-done.9.refs_2_, ...), custom_call_target="tpu_custom_call", output_to_operand_aliasing={{}: (20, {})} | custom-call | tf_op jit(solution)/shard_map/pallas_call | solution.py:297
  157.1 2.3 %shard_map.113.refs_9_ = f32[3,4,256,256]{3,2,1,0:T(8,128)S(1)} custom-call(s32[2]{0:T(128)S(1)} %pad_add_fusion.me_ref, bf16[192,256]{1,0:T(8,128)(2,1)S(1)} %get-tuple-element.97.refs_0_, bf16[192,256]{1,0:T(8,128)(2,1)S(1)} %collective-permute-done.22.refs_1_, bf16[192,256]{1,0:T(8,128)(2,1)S(1)} %collective-permute-done.23.refs_2_, ...), custom_call_target="tpu_custom_call" | custom-call | tf_op jit(solution)/shard_map/pallas_call | solution.py:297
  159.5 3.8 %shard_map.114 = f32[2,2,256,1536]{3,2,1,0:T(8,128)} custom-call(s32[2]{0:T(128)S(1)} %pad_add_fusion.me_ref, bf16[192,256]{1,0:T(8,128)(2,1)S(1)} %get-tuple-element.105.refs_0_, bf16[192,256]{1,0:T(8,128)(2,1)S(1)} %collective-permute-done.29.refs_1_, bf16[192,256]{1,0:T(8,128)(2,1)S(1)} %collective-permute-done.30.refs_2_, ...), custom_call_target="tpu_custom_call", output_to_operand_aliasing={{}: (12, {})} | custom-call | tf_op jit(solution)/shard_map/pallas_call | solution.py:297
  (75 shorter events, 6.3 us)
Async XLA Ops:
  0.9 8.2 %copy-start = (bf16[256,192,2,128]{3,2,1,0:T(2,128)(2,1)S(1)}, bf16[256,192,2,128]{3,2,1,0:T(2,128)(2,1)}, u32[]{:S(2)}) copy-start(bf16[256,192,2,128]{3,2,1,0:T(2,128)(2,1)} %param.10) | copy-start | bytes 75497472
  9.1 2.2 %copy-start.1 = (bf16[64,128,256]{2,1,0:T(8,128)(2,1)S(1)}, bf16[64,128,256]{2,1,0:T(8,128)(2,1)}, u32[]{:S(2)}) copy-start(bf16[64,128,256]{2,1,0:T(8,128)(2,1)} %ker.15) | copy-start | bytes 12582916
  11.3 6.6 %slice-start = ((s8[25165824]{0:T(1024)(128)(4,1)}), s8[4194304]{0:T(1024)(128)(4,1)S(1)}, s32[]{:S(2)}) async-start(s8[25165824]{0:T(1024)(128)(4,1)} %bitcast.20), calls=%async_computation | async-start | bytes 8388608
  11.3 6.6 %slice-start.1 = ((s8[25165824]{0:T(1024)(128)(4,1)}), s8[4194304]{0:T(1024)(128)(4,1)S(1)}, s32[]{:S(2)}) async-start(s8[25165824]{0:T(1024)(128)(4,1)} %bitcast.20), calls=%async_computation.1 | async-start | bytes 8388608
  11.3 6.6 %slice-start.2 = ((s8[25165824]{0:T(1024)(128)(4,1)}), s8[4194304]{0:T(1024)(128)(4,1)S(1)}, s32[]{:S(2)}) async-start(s8[25165824]{0:T(1024)(128)(4,1)} %bitcast.20), calls=%async_computation.2 | async-start | bytes 8388608
  14.0 3.9 %slice-start.3 = ((s8[25165824]{0:T(1024)(128)(4,1)}), s8[4194304]{0:T(1024)(128)(4,1)S(1)}, s32[]{:S(2)}) async-start(s8[25165824]{0:T(1024)(128)(4,1)} %bitcast.20), calls=%async_computation.3 | async-start | bytes 8388608
  14.0 4.5 %slice-start.4 = ((s8[25165824]{0:T(1024)(128)(4,1)}), s8[4194304]{0:T(1024)(128)(4,1)S(1)}, s32[]{:S(2)}) async-start(s8[25165824]{0:T(1024)(128)(4,1)} %bitcast.20), calls=%async_computation.4 | async-start | bytes 8388608
  14.1 5.7 %slice-start.5 = ((s8[25165824]{0:T(1024)(128)(4,1)}), s8[4194304]{0:T(1024)(128)(4,1)S(1)}, s32[]{:S(2)}) async-start(s8[25165824]{0:T(1024)(128)(4,1)} %bitcast.20), calls=%async_computation.5 | async-start | bytes 8388608
  14.1 3.6 %collective-permute-start = (bf16[2,8,192,256]{3,2,1,0:T(8,128)(2,1)S(1)}, bf16[2,8,192,256]{3,2,1,0:T(8,128)(2,1)S(1)}, u32[]{:S(2)}, u32[]{:S(2)}) collective-permute-start(bf16[2,8,192,256]{3,2,1,0:T(8,128)(2,1)S(1)} %shard_map.100), channel_id=1, source_target_pairs={{0,1},{1,0},{2,3},{3,2},{4,5},{5,4},{6,7},{7,6},{8,9},{9,8},{10,11... | collective-permute-start | bytes 4718600 | tf_op jit(solution)/shard_map/ppermute | solution.py:358
  22.5 9.1 %collective-permute-start.1 = (bf16[2,8,192,256]{3,2,1,0:T(8,128)(2,1)S(1)}, bf16[2,8,192,256]{3,2,1,0:T(8,128)(2,1)S(1)}, u32[]{:S(2)}, u32[]{:S(2)}) collective-permute-start(bf16[2,8,192,256]{3,2,1,0:T(8,128)(2,1)S(1)} %shard_map.102), channel_id=1, source_target_pairs={{0,1},{1,0},{2,3},{3,2},{4,5},{5,4},{6,7},{7,6},{8,9},{9,8},{10,11... | collective-permute-start | bytes 4718600 | tf_op jit(solution)/shard_map/ppermute | solution.py:358
  28.5 6.0 %collective-permute-start.2 = (bf16[2,8,192,256]{3,2,1,0:T(8,128)(2,1)S(1)}, bf16[2,8,192,256]{3,2,1,0:T(8,128)(2,1)S(1)}, u32[]{:S(2)}, u32[]{:S(2)}) collective-permute-start(bf16[2,8,192,256]{3,2,1,0:T(8,128)(2,1)S(1)} %shard_map.104), channel_id=1, source_target_pairs={{0,1},{1,0},{2,3},{3,2},{4,5},{5,4},{6,7},{7,6},{8,9},{9,8},{10,11... | collective-permute-start | bytes 4718600 | tf_op jit(solution)/shard_map/ppermute | solution.py:358
  28.6 20.8 %collective-permute-start.3 = (bf16[8,192,256]{2,1,0:T(8,128)(2,1)S(1)}, bf16[8,192,256]{2,1,0:T(8,128)(2,1)S(1)}, u32[]{:S(2)}, u32[]{:S(2)}) collective-permute-start(bf16[8,192,256]{2,1,0:T(8,128)(2,1)S(1)} %fusion), channel_id=1, source_target_pairs={{0,2},{1,3},{2,0},{3,1},{4,6},{5,7},{6,4},{7,5},{8,10},{9,11},{10,... | collective-permute-start | bytes 2359304 | tf_op jit(solution)/shard_map/ppermute | solution.py:364
  53.0 24.1 %collective-permute-start.5 = (bf16[2,8,192,256]{3,2,1,0:T(8,128)(2,1)S(1)}, bf16[2,8,192,256]{3,2,1,0:T(8,128)(2,1)S(1)}, u32[]{:S(2)}, u32[]{:S(2)}) collective-permute-start(bf16[2,8,192,256]{3,2,1,0:T(8,128)(2,1)S(1)} %shard_map.107), channel_id=1, source_target_pairs={{0,1},{1,0},{2,3},{3,2},{4,5},{5,4},{6,7},{7,6},{8,9},{9,8},{10,11... | collective-permute-start | bytes 4718600 | tf_op jit(solution)/shard_map/ppermute | solution.py:358
  53.0 20.5 %collective-permute-start.4 = (bf16[8,192,256]{2,1,0:T(8,128)(2,1)S(1)}, bf16[8,192,256]{2,1,0:T(8,128)(2,1)S(1)}, u32[]{:S(2)}, u32[]{:S(2)}) collective-permute-start(bf16[8,192,256]{2,1,0:T(8,128)(2,1)S(1)} %fusion.1), channel_id=1, source_target_pairs={{0,2},{1,3},{2,0},{3,1},{4,6},{5,7},{6,4},{7,5},{8,10},{9,11},{10,... | collective-permute-start | bytes 2359304 | tf_op jit(solution)/shard_map/ppermute | solution.py:364
  54.8 49.7 %collective-permute-start.6 = (bf16[8,192,256]{2,1,0:T(8,128)(2,1)S(1)}, bf16[8,192,256]{2,1,0:T(8,128)(2,1)S(1)}, u32[]{:S(2)}, u32[]{:S(2)}) collective-permute-start(bf16[8,192,256]{2,1,0:T(8,128)(2,1)S(1)} %fusion.2), channel_id=1, source_target_pairs={{0,2},{1,3},{2,0},{3,1},{4,6},{5,7},{6,4},{7,5},{8,10},{9,11},{10,... | collective-permute-start | bytes 2359304 | tf_op jit(solution)/shard_map/ppermute | solution.py:364
  77.3 46.2 %collective-permute-start.7 = (bf16[8,192,256]{2,1,0:T(8,128)(2,1)S(1)}, bf16[8,192,256]{2,1,0:T(8,128)(2,1)S(1)}, u32[]{:S(2)}, u32[]{:S(2)}) collective-permute-start(bf16[8,192,256]{2,1,0:T(8,128)(2,1)S(1)} %fusion.3), channel_id=1, source_target_pairs={{0,2},{1,3},{2,0},{3,1},{4,6},{5,7},{6,4},{7,5},{8,10},{9,11},{10,... | collective-permute-start | bytes 2359304 | tf_op jit(solution)/shard_map/ppermute | solution.py:364
  79.1 4.7 %collective-permute-start.8 = (bf16[192,256]{1,0:T(8,128)(2,1)S(1)}, bf16[192,256]{1,0:T(8,128)(2,1)S(1)}, u32[]{:S(2)}, u32[]{:S(2)}) collective-permute-start(bf16[192,256]{1,0:T(8,128)(2,1)S(1)} %get-tuple-element.82), channel_id=1, source_target_pairs={{0,4},{4,0},{8,12},{12,8},{16,20},{20,16},{24,28},{28,24},{1,5},{5... | collective-permute-start | bytes 294920 | tf_op jit(solution)/shard_map/ppermute | solution.py:375
  80.6 5.8 %collective-permute-start.9 = (bf16[192,256]{1,0:T(8,128)(2,1)S(1)}, bf16[192,256]{1,0:T(8,128)(2,1)S(1)}, u32[]{:S(2)}, u32[]{:S(2)}) collective-permute-start(bf16[192,256]{1,0:T(8,128)(2,1)S(1)} %get-tuple-element.83), channel_id=1, source_target_pairs={{0,8},{4,12},{8,0},{12,4},{16,24},{20,28},{24,16},{28,20},{1,9},{5... | collective-permute-start | bytes 294920 | tf_op jit(solution)/shard_map/ppermute | solution.py:375
  82.2 6.6 %collective-permute-start.10 = (bf16[192,256]{1,0:T(8,128)(2,1)S(1)}, bf16[192,256]{1,0:T(8,128)(2,1)S(1)}, u32[]{:S(2)}, u32[]{:S(2)}) collective-permute-start(bf16[192,256]{1,0:T(8,128)(2,1)S(1)} %get-tuple-element.84), channel_id=1, source_target_pairs={{0,12},{4,8},{8,4},{12,0},{16,28},{20,24},{24,20},{28,16},{1,13},{... | collective-permute-start | bytes 294920 | tf_op jit(solution)/shard_map/ppermute | solution.py:375
  83.8 12.8 %collective-permute-start.11 = (bf16[192,256]{1,0:T(8,128)(2,1)S(1)}, bf16[192,256]{1,0:T(8,128)(2,1)S(1)}, u32[]{:S(2)}, u32[]{:S(2)}) collective-permute-start(bf16[192,256]{1,0:T(8,128)(2,1)S(1)} %get-tuple-element.85), channel_id=1, source_target_pairs={{0,16},{4,20},{8,24},{12,28},{16,0},{20,4},{24,8},{28,12},{1,17},{... | collective-permute-start | bytes 294920 | tf_op jit(solution)/shard_map/ppermute | solution.py:375
  86.4 14.0 %collective-permute-start.12 = (bf16[192,256]{1,0:T(8,128)(2,1)S(1)}, bf16[192,256]{1,0:T(8,128)(2,1)S(1)}, u32[]{:S(2)}, u32[]{:S(2)}) collective-permute-start(bf16[192,256]{1,0:T(8,128)(2,1)S(1)} %get-tuple-element.86), channel_id=1, source_target_pairs={{0,20},{4,16},{8,28},{12,24},{16,4},{20,0},{24,12},{28,8},{1,21},{... | collective-permute-start | bytes 294920 | tf_op jit(solution)/shard_map/ppermute | solution.py:375
  88.8 11.9 %collective-permute-start.13 = (bf16[192,256]{1,0:T(8,128)(2,1)S(1)}, bf16[192,256]{1,0:T(8,128)(2,1)S(1)}, u32[]{:S(2)}, u32[]{:S(2)}) collective-permute-start(bf16[192,256]{1,0:T(8,128)(2,1)S(1)} %get-tuple-element.87), channel_id=1, source_target_pairs={{0,24},{4,28},{8,16},{12,20},{16,8},{20,12},{24,0},{28,4},{1,25},{... | collective-permute-start | bytes 294920 | tf_op jit(solution)/shard_map/ppermute | solution.py:375
  96.6 8.0 %collective-permute-start.14 = (bf16[192,256]{1,0:T(8,128)(2,1)S(1)}, bf16[192,256]{1,0:T(8,128)(2,1)S(1)}, u32[]{:S(2)}, u32[]{:S(2)}) collective-permute-start(bf16[192,256]{1,0:T(8,128)(2,1)S(1)} %get-tuple-element.88), channel_id=1, source_target_pairs={{0,28},{4,24},{8,20},{12,16},{16,12},{20,8},{24,4},{28,0},{1,29},{... | collective-permute-start | bytes 294920 | tf_op jit(solution)/shard_map/ppermute | solution.py:375
  100.4 8.1 %collective-permute-start.15 = (bf16[192,256]{1,0:T(8,128)(2,1)S(1)}, bf16[192,256]{1,0:T(8,128)(2,1)S(1)}, u32[]{:S(2)}, u32[]{:S(2)}) collective-permute-start(bf16[192,256]{1,0:T(8,128)(2,1)S(1)} %get-tuple-element.89), channel_id=1, source_target_pairs={{0,4},{4,0},{8,12},{12,8},{16,20},{20,16},{24,28},{28,24},{1,5},{5... | collective-permute-start | bytes 294920 | tf_op jit(solution)/shard_map/ppermute | solution.py:375
  100.7 7.8 %collective-permute-start.16 = (bf16[192,256]{1,0:T(8,128)(2,1)S(1)}, bf16[192,256]{1,0:T(8,128)(2,1)S(1)}, u32[]{:S(2)}, u32[]{:S(2)}) collective-permute-start(bf16[192,256]{1,0:T(8,128)(2,1)S(1)} %get-tuple-element.90), channel_id=1, source_target_pairs={{0,8},{4,12},{8,0},{12,4},{16,24},{20,28},{24,16},{28,20},{1,9},{5... | collective-permute-start | bytes 294920 | tf_op jit(solution)/shard_map/ppermute | solution.py:375
  104.6 7.2 %collective-permute-start.17 = (bf16[192,256]{1,0:T(8,128)(2,1)S(1)}, bf16[192,256]{1,0:T(8,128)(2,1)S(1)}, u32[]{:S(2)}, u32[]{:S(2)}) collective-permute-start(bf16[192,256]{1,0:T(8,128)(2,1)S(1)} %get-tuple-element.91), channel_id=1, source_target_pairs={{0,12},{4,8},{8,4},{12,0},{16,28},{20,24},{24,20},{28,16},{1,13},{... | collective-permute-start | bytes 294920 | tf_op jit(solution)/shard_map/ppermute | solution.py:375
  104.6 13.4 %collective-permute-start.18 = (bf16[192,256]{1,0:T(8,128)(2,1)S(1)}, bf16[192,256]{1,0:T(8,128)(2,1)S(1)}, u32[]{:S(2)}, u32[]{:S(2)}) collective-permute-start(bf16[192,256]{1,0:T(8,128)(2,1)S(1)} %get-tuple-element.92), channel_id=1, source_target_pairs={{0,16},{4,20},{8,24},{12,28},{16,0},{20,4},{24,8},{28,12},{1,17},{... | collective-permute-start | bytes 294920 | tf_op jit(solution)/shard_map/ppermute | solution.py:375
  108.5 12.4 %collective-permute-start.19 = (bf16[192,256]{1,0:T(8,128)(2,1)S(1)}, bf16[192,256]{1,0:T(8,128)(2,1)S(1)}, u32[]{:S(2)}, u32[]{:S(2)}) collective-permute-start(bf16[192,256]{1,0:T(8,128)(2,1)S(1)} %get-tuple-element.93), channel_id=1, source_target_pairs={{0,20},{4,16},{8,28},{12,24},{16,4},{20,0},{24,12},{28,8},{1,21},{... | collective-permute-start | bytes 294920 | tf_op jit(solution)/shard_map/ppermute | solution.py:375
  108.5 15.6 %copy-start.2 = (f32[4,48,384]{2,1,0:T(8,128)S(1)}, f32[4,48,384]{2,1,0:T(8,128)}, u32[]{:S(2)}) copy-start(f32[4,48,384]{2,1,0:T(8,128)} %constant.20.clone.vs_ref) | copy-start | bytes 884740
  108.5 15.6 %copy-start.3 = (f32[4,48,384]{2,1,0:T(8,128)S(1)}, f32[4,48,384]{2,1,0:T(8,128)}, u32[]{:S(2)}) copy-start(f32[4,48,384]{2,1,0:T(8,128)} %constant.19.clone.vc_ref) | copy-start | bytes 884740
  108.5 15.6 %copy-start.5 = (f32[8,384]{1,0:T(8,128)S(1)}, f32[8,384]{1,0:T(8,128)}, u32[]{:S(2)}) copy-start(f32[8,384]{1,0:T(8,128)} %constant.17.clone.uc_ref) | copy-start | bytes 36868
  108.6 15.6 %copy-start.6 = (f32[8,384]{1,0:T(8,128)S(1)}, f32[8,384]{1,0:T(8,128)}, u32[]{:S(2)}) copy-start(f32[8,384]{1,0:T(8,128)} %constant.18.clone.us_ref) | copy-start | bytes 36868
  108.6 12.3 %collective-permute-start.20 = (bf16[192,256]{1,0:T(8,128)(2,1)S(1)}, bf16[192,256]{1,0:T(8,128)(2,1)S(1)}, u32[]{:S(2)}, u32[]{:S(2)}) collective-permute-start(bf16[192,256]{1,0:T(8,128)(2,1)S(1)} %get-tuple-element.94), channel_id=1, source_target_pairs={{0,24},{4,28},{8,16},{12,20},{16,8},{20,12},{24,0},{28,4},{1,25},{... | collective-permute-start | bytes 294920 | tf_op jit(solution)/shard_map/ppermute | solution.py:375
  111.8 14.4 %collective-permute-start.21 = (bf16[192,256]{1,0:T(8,128)(2,1)S(1)}, bf16[192,256]{1,0:T(8,128)(2,1)S(1)}, u32[]{:S(2)}, u32[]{:S(2)}) collective-permute-start(bf16[192,256]{1,0:T(8,128)(2,1)S(1)} %get-tuple-element.95), channel_id=1, source_target_pairs={{0,28},{4,24},{8,20},{12,16},{16,12},{20,8},{24,4},{28,0},{1,29},{... | collective-permute-start | bytes 294920 | tf_op jit(solution)/shard_map/ppermute | solution.py:375
  118.0 11.7 %collective-permute-start.22 = (bf16[192,256]{1,0:T(8,128)(2,1)S(1)}, bf16[192,256]{1,0:T(8,128)(2,1)S(1)}, u32[]{:S(2)}, u32[]{:S(2)}) collective-permute-start(bf16[192,256]{1,0:T(8,128)(2,1)S(1)} %get-tuple-element.98), channel_id=1, source_target_pairs={{0,4},{4,0},{8,12},{12,8},{16,20},{20,16},{24,28},{28,24},{1,5},{5... | collective-permute-start | bytes 294920 | tf_op jit(solution)/shard_map/ppermute | solution.py:375
  120.9 10.7 %collective-permute-start.23 = (bf16[192,256]{1,0:T(8,128)(2,1)S(1)}, bf16[192,256]{1,0:T(8,128)(2,1)S(1)}, u32[]{:S(2)}, u32[]{:S(2)}) collective-permute-start(bf16[192,256]{1,0:T(8,128)(2,1)S(1)} %get-tuple-element.99), channel_id=1, source_target_pairs={{0,8},{4,12},{8,0},{12,4},{16,24},{20,28},{24,16},{28,20},{1,9},{5... | collective-permute-start | bytes 294920 | tf_op jit(solution)/shard_map/ppermute | solution.py:375
  120.9 12.4 %collective-permute-start.24 = (bf16[192,256]{1,0:T(8,128)(2,1)S(1)}, bf16[192,256]{1,0:T(8,128)(2,1)S(1)}, u32[]{:S(2)}, u32[]{:S(2)}) collective-permute-start(bf16[192,256]{1,0:T(8,128)(2,1)S(1)} %get-tuple-element.100), channel_id=1, source_target_pairs={{0,12},{4,8},{8,4},{12,0},{16,28},{20,24},{24,20},{28,16},{1,13},{... | collective-permute-start | bytes 294920 | tf_op jit(solution)/shard_map/ppermute | solution.py:375
  123.5 11.5 %collective-permute-start.25 = (bf16[192,256]{1,0:T(8,128)(2,1)S(1)}, bf16[192,256]{1,0:T(8,128)(2,1)S(1)}, u32[]{:S(2)}, u32[]{:S(2)}) collective-permute-start(bf16[192,256]{1,0:T(8,128)(2,1)S(1)} %get-tuple-element.101), channel_id=1, source_target_pairs={{0,16},{4,20},{8,24},{12,28},{16,0},{20,4},{24,8},{28,12},{1,17},{... | collective-permute-start | bytes 294920 | tf_op jit(solution)/shard_map/ppermute | solution.py:375
  126.2 14.2 %collective-permute-start.26 = (bf16[192,256]{1,0:T(8,128)(2,1)S(1)}, bf16[192,256]{1,0:T(8,128)(2,1)S(1)}, u32[]{:S(2)}, u32[]{:S(2)}) collective-permute-start(bf16[192,256]{1,0:T(8,128)(2,1)S(1)} %get-tuple-element.102), channel_id=1, source_target_pairs={{0,20},{4,16},{8,28},{12,24},{16,4},{20,0},{24,12},{28,8},{1,21},{... | collective-permute-start | bytes 294920 | tf_op jit(solution)/shard_map/ppermute | solution.py:375
  129.7 10.7 %collective-permute-start.27 = (bf16[192,256]{1,0:T(8,128)(2,1)S(1)}, bf16[192,256]{1,0:T(8,128)(2,1)S(1)}, u32[]{:S(2)}, u32[]{:S(2)}) collective-permute-start(bf16[192,256]{1,0:T(8,128)(2,1)S(1)} %get-tuple-element.103), channel_id=1, source_target_pairs={{0,24},{4,28},{8,16},{12,20},{16,8},{20,12},{24,0},{28,4},{1,25},{... | collective-permute-start | bytes 294920 | tf_op jit(solution)/shard_map/ppermute | solution.py:375
  131.6 11.8 %collective-permute-start.28 = (bf16[192,256]{1,0:T(8,128)(2,1)S(1)}, bf16[192,256]{1,0:T(8,128)(2,1)S(1)}, u32[]{:S(2)}, u32[]{:S(2)}) collective-permute-start(bf16[192,256]{1,0:T(8,128)(2,1)S(1)} %get-tuple-element.104), channel_id=1, source_target_pairs={{0,28},{4,24},{8,20},{12,16},{16,12},{20,8},{24,4},{28,0},{1,29},{... | collective-permute-start | bytes 294920 | tf_op jit(solution)/shard_map/ppermute | solution.py:375
  133.3 17.0 %collective-permute-start.29 = (bf16[192,256]{1,0:T(8,128)(2,1)S(1)}, bf16[192,256]{1,0:T(8,128)(2,1)S(1)}, u32[]{:S(2)}, u32[]{:S(2)}) collective-permute-start(bf16[192,256]{1,0:T(8,128)(2,1)S(1)} %get-tuple-element.106), channel_id=1, source_target_pairs={{0,4},{4,0},{8,12},{12,8},{16,20},{20,16},{24,28},{28,24},{1,5},{5... | collective-permute-start | bytes 294920 | tf_op jit(solution)/shard_map/ppermute | solution.py:375
  135.0 15.4 %collective-permute-start.30 = (bf16[192,256]{1,0:T(8,128)(2,1)S(1)}, bf16[192,256]{1,0:T(8,128)(2,1)S(1)}, u32[]{:S(2)}, u32[]{:S(2)}) collective-permute-start(bf16[192,256]{1,0:T(8,128)(2,1)S(1)} %get-tuple-element.107), channel_id=1, source_target_pairs={{0,8},{4,12},{8,0},{12,4},{16,24},{20,28},{24,16},{28,20},{1,9},{5... | collective-permute-start | bytes 294920 | tf_op jit(solution)/shard_map/ppermute | solution.py:375
  140.4 19.0 %collective-permute-start.31 = (bf16[192,256]{1,0:T(8,128)(2,1)S(1)}, bf16[192,256]{1,0:T(8,128)(2,1)S(1)}, u32[]{:S(2)}, u32[]{:S(2)}) collective-permute-start(bf16[192,256]{1,0:T(8,128)(2,1)S(1)} %get-tuple-element.108), channel_id=1, source_target_pairs={{0,12},{4,8},{8,4},{12,0},{16,28},{20,24},{24,20},{28,16},{1,13},{... | collective-permute-start | bytes 294920 | tf_op jit(solution)/shard_map/ppermute | solution.py:375
  140.4 19.0 %collective-permute-start.32 = (bf16[192,256]{1,0:T(8,128)(2,1)S(1)}, bf16[192,256]{1,0:T(8,128)(2,1)S(1)}, u32[]{:S(2)}, u32[]{:S(2)}) collective-permute-start(bf16[192,256]{1,0:T(8,128)(2,1)S(1)} %get-tuple-element.109), channel_id=1, source_target_pairs={{0,16},{4,20},{8,24},{12,28},{16,0},{20,4},{24,8},{28,12},{1,17},{... | collective-permute-start | bytes 294920 | tf_op jit(solution)/shard_map/ppermute | solution.py:375
  143.4 16.0 %collective-permute-start.33 = (bf16[192,256]{1,0:T(8,128)(2,1)S(1)}, bf16[192,256]{1,0:T(8,128)(2,1)S(1)}, u32[]{:S(2)}, u32[]{:S(2)}) collective-permute-start(bf16[192,256]{1,0:T(8,128)(2,1)S(1)} %get-tuple-element.110), channel_id=1, source_target_pairs={{0,20},{4,16},{8,28},{12,24},{16,4},{20,0},{24,12},{28,8},{1,21},{... | collective-permute-start | bytes 294920 | tf_op jit(solution)/shard_map/ppermute | solution.py:375
  150.3 9.2 %collective-permute-start.34 = (bf16[192,256]{1,0:T(8,128)(2,1)S(1)}, bf16[192,256]{1,0:T(8,128)(2,1)S(1)}, u32[]{:S(2)}, u32[]{:S(2)}) collective-permute-start(bf16[192,256]{1,0:T(8,128)(2,1)S(1)} %get-tuple-element.111), channel_id=1, source_target_pairs={{0,24},{4,28},{8,16},{12,20},{16,8},{20,12},{24,0},{28,4},{1,25},{... | collective-permute-start | bytes 294920 | tf_op jit(solution)/shard_map/ppermute | solution.py:375
  150.4 9.0 %collective-permute-start.35 = (bf16[192,256]{1,0:T(8,128)(2,1)S(1)}, bf16[192,256]{1,0:T(8,128)(2,1)S(1)}, u32[]{:S(2)}, u32[]{:S(2)}) collective-permute-start(bf16[192,256]{1,0:T(8,128)(2,1)S(1)} %get-tuple-element.112), channel_id=1, source_target_pairs={{0,28},{4,24},{8,20},{12,16},{16,12},{20,8},{24,4},{28,0},{1,29},{... | collective-permute-start | bytes 294920 | tf_op jit(solution)/shard_map/ppermute | solution.py:375
  (1 other events, 1.6 us)
